TPU v7x, 32 devices: a whole 2x2x4 slice. The times are simulated.
32 devices in a mesh: arrays: 2 (over y), chan: 4 (over z), win: 4 (over x, core).
Axes of the slice: x: 2, y: 2, z: 4, core: 2. Of those that a mesh axis runs over, the one named last changes fastest.
Arguments:
- traces: float32 [16, 4, 12, 2048], P(('arrays', 'chan'), 'win'), parts along dimension 0
- seg_count: int32 [8], P('arrays'), parts along dimension 0, may hold values from 1 to 12, as said below
Outputs:
- stacked: float32 [8, 2, 2, 2, 1024], P(('arrays', 'chan')), parts along dimension 0
There are 2 independent parts, one for each index of `arrays`. A program takes and returns all parts, laid end to end along the dimension named above; each array names one. Nothing has to cross between parts.
Inputs may be any that keep to these rules, and one draw needn't show every extreme that they name: `seg_count`: every sub-window keeps at least one segment, and some sub-window keeps all 12.
All inputs are finite; a program needn't handle non-finite values.
Results may differ from a plain program's by a relative error of at most 0.0068.
Values may be sent and summed in bfloat16 or wider, within the bound.
No kernel may reach another device: no remote copies, remote signals or barrier semaphores. Data moves between devices by JAX's collectives and lax.ppermute only.
A program may use at most 64 MiB of HBM per device.

v0:
```python
import math

import jax
import jax.numpy as jnp
from jax import lax
from jax.sharding import PartitionSpec as P

NFFT = 2048
F = 512
LAGS = 1024


def passed_along(array, axis, by):
    length = lax.axis_size(axis)
    return lax.ppermute(array, axis, [(i, (i + by) % length) for i in range(length)])


def forward_table(length, bin_count, lowest_bin):
    sample_index = jnp.arange(length, dtype=jnp.int32)
    bin_index = jnp.arange(bin_count, dtype=jnp.int32) + lowest_bin
    phase_index = sample_index[:, None] * bin_index[None, :] % length
    angles = phase_index.astype(jnp.float32) * (2.0 * math.pi / length)
    return jnp.concatenate([jnp.cos(angles), -jnp.sin(angles)], axis=1)


def inverse_table(length, bin_count, lowest_bin, lag_count):
    bin_index = jnp.arange(bin_count, dtype=jnp.int32) + lowest_bin
    shifts = (jnp.arange(lag_count, dtype=jnp.int32) - lag_count // 2 + length) % length
    phase_index = bin_index[:, None] * shifts[None, :] % length
    angles = phase_index.astype(jnp.float32) * (2.0 * math.pi / length)
    cosine = jnp.cos(angles)
    sine_part = jnp.sin(angles)
    upper_rows = jnp.concatenate([cosine, sine_part], axis=1)
    lower_rows = jnp.concatenate([-sine_part, cosine], axis=1)
    joined = jnp.concatenate([upper_rows, lower_rows], axis=0) / math.sqrt(bin_count)
    return joined.astype(jnp.bfloat16)


def whiten(series, dft_table, bin_count):
    spectra = jnp.dot(
        series, dft_table, precision=lax.Precision.HIGHEST, preferred_element_type=jnp.float32
    )
    real_part = spectra[:, :bin_count]
    imag_part = spectra[:, bin_count:]
    spectral_power = real_part * real_part + imag_part * imag_part
    rms_level = jnp.sqrt(jnp.mean(spectral_power, axis=1, keepdims=True) + 1e-06)
    divisor = jnp.maximum(jnp.sqrt(spectral_power), 0.3 * rms_level)
    return (spectra / jnp.concatenate([divisor, divisor], axis=1)).astype(jnp.bfloat16)


def cross_spectra(left_spectra, right_spectra, bin_count):
    left_float = left_spectra.astype(jnp.float32)
    right_float = right_spectra.astype(jnp.float32)
    left_real = left_float[:, None, :, None, :bin_count]
    left_imag = left_float[:, None, :, None, bin_count:]
    right_real = right_float[:, :, None, :, :bin_count]
    right_imag = right_float[:, :, None, :, bin_count:]
    cross_real = left_real * right_real + left_imag * right_imag
    cross_imag = left_imag * right_real - left_real * right_imag
    return jnp.concatenate([cross_real, cross_imag], axis=-1).astype(jnp.bfloat16)


def phase_sums(correlated, seg_weights, lag_count):
    direct = correlated[..., :lag_count]
    quadrature = correlated[..., lag_count:]
    magnitude = jnp.sqrt(direct * direct + quadrature * quadrature)
    divisor = jnp.maximum(magnitude, 0.5)
    weighting = seg_weights[:, None, None]
    linear = jnp.sum(weighting * direct, axis=0)
    cos_sum = jnp.sum(weighting * (direct / divisor), axis=0)
    sin_sum = jnp.sum(weighting * (quadrature / divisor), axis=0)
    return (linear, cos_sum, sin_sum)


def accumulate(left_spectra, right_spectra, seg_weights, backward):
    products = cross_spectra(left_spectra, right_spectra, F)
    rows = products.shape[0]
    pair_count = products.shape[1] * products.shape[2] * products.shape[3]
    linear = jnp.zeros((pair_count, LAGS), jnp.float32)
    cos_sum = jnp.zeros((pair_count, LAGS), jnp.float32)
    sin_sum = jnp.zeros((pair_count, LAGS), jnp.float32)
    for seg_start in range(0, rows, 4):
        row_block = products[seg_start : seg_start + 4].reshape(-1, 2 * F)
        correlated = jnp.dot(row_block, backward, preferred_element_type=jnp.float32).reshape(
            4, pair_count, 2 * LAGS
        )
        part_linear, part_cos, part_sin = phase_sums(
            correlated, seg_weights[seg_start : seg_start + 4], LAGS
        )
        linear = linear + part_linear
        cos_sum = cos_sum + part_cos
        sin_sum = sin_sum + part_sin
    return (linear, cos_sum, sin_sum)


def shards(traces, seg_count):
    lowest_bin = NFFT // 16
    forward = forward_table(NFFT, F, lowest_bin)
    backward = inverse_table(NFFT, F, lowest_bin, LAGS)
    channels = traces.shape[0]
    segments = traces.shape[2]
    own_spectra = whiten(traces.reshape(-1, NFFT), forward, F).reshape(channels, segments, 2 * F)
    span_blocks = lax.axis_size("chan") // 2
    kept_total = jnp.sum(seg_count).astype(jnp.float32)
    collected = own_spectra[None]
    held_blocks = 1
    while held_blocks < span_blocks:
        sent_blocks = min(held_blocks, span_blocks - held_blocks)
        arrived = passed_along(collected, "chan", -held_blocks)
        collected = jnp.concatenate([collected, arrived], axis=0)
        held_blocks = held_blocks + sent_blocks
    opposite_block = passed_along(own_spectra[None], "chan", -span_blocks)
    visitors = jnp.concatenate([collected[1:], opposite_block], axis=0)
    window = lax.axis_index("win")
    positions = jnp.arange(seg_count.shape[0], dtype=jnp.int32)
    kept_count = jnp.sum(jnp.where(positions == window, seg_count, 0))
    seg_weights = (jnp.arange(segments, dtype=jnp.int32) < kept_count).astype(jnp.float32)
    linear, cos_sum, sin_sum = accumulate(
        own_spectra.transpose(1, 0, 2), visitors.transpose(2, 0, 1, 3), seg_weights, backward
    )
    linear, cos_sum, sin_sum = lax.psum((linear, cos_sum, sin_sum), "win")
    result = linear * (cos_sum * cos_sum + sin_sum * sin_sum) / (kept_total * kept_total)
    return result.reshape(1, span_blocks, channels, channels, LAGS)


def solution(mesh):
    placed = (P(("arrays", "chan"), "win", None, None), P("arrays"))
    return jax.shard_map(
        shards,
        mesh=mesh,
        in_specs=placed,
        out_specs=P(("arrays", "chan"), None, None, None, None),
        check_vma=False,
    )
```

profile of v0, /device:TPU:0, one launch (start us, length us, event | category | flops | bytes accessed | tf_op | source)
XLA Modules:
  0.0 107.0 jit_solution(3016193065485282776)
XLA Ops:
  6.5 0.0 all-reduce.3.cloned.1.call-start
  6.5 0.0 copy-start.1
  6.5 18.0 %fusion.15 = (f32[2048,512]{1,0:T(8,128)}, f32[2048,512]{1,0:T(8,128)}) fusion(s32[512]{0:T(512)S(1)} %iota_add_fusion), kind=kLoop, calls=%fused_computation.25 | loop fusion | flops 15728640 | bytes 8390656 | tf_op jit(solution)/shard_map/cos | solution.py:23
  24.6 0.0 copy-done.1
  24.6 0.5 reduce
  25.1 6.8 %fusion.16 = f32[24,1024]{1,0:T(8,128)S(1)} fusion(f32[24,2048]{1,0:T(8,128)S(1)} %reshape.61, f32[2048,512]{1,0:T(8,128)} %get-tuple-element.32, f32[2048,512]{1,0:T(8,128)} %get-tuple-element.31), kind=kOutput, calls=%fused_computation.26 | convolution fusion | flops 606076928 | bytes 8683520 | tf_op jit(solution)/shard_map/dot_general | solution.py:40
  31.9 0.0 copy-start.2
  31.9 0.1 fusion.26
  32.1 0.1 sqrt_maximum_fusion.3
  32.2 5.1 %collective-permute-start = (bf16[1,2,12,1024]{3,2,1,0:T(8,128)(2,1)S(1)}, bf16[1,2,12,1024]{3,2,1,0:T(8,128)(2,1)S(1)}, u32[]{:S(2)}, u32[]{:S(2)}) collective-permute-start(bf16[1,2,12,1024]{3,2,1,0:T(8,128)(2,1)S(1)} %broadcast_in_dim_reshape.4), channel_id=1, source_target_pairs={{0,12},{4,0},{8,4},{12,8},{1,13},{5,1},{9,5},{13,9},{2,14},{6,2},{... | collective-permute-start | bytes 147464 | tf_op jit(solution)/shard_map/ppermute | solution.py:15
  37.3 0.0 collective-permute-start.1
  37.4 9.8 %fusion.19 = (f32[512,1024]{1,0:T(8,128)S(1)}, f32[512,1024]{1,0:T(8,128)}, f32[512,1024]{1,0:T(8,128)}) fusion(s32[1024]{0:T(1024)S(1)} %add_select_fusion.2, s32[512]{0:T(512)S(1)} %iota_add_fusion), kind=kLoop, calls=%fused_computation.27 | loop fusion | flops 7864320 | bytes 6297600 | tf_op jit(solution)/shard_map/sin | solution.py:32
  47.2 0.0 copy-done.2
  47.2 0.6 fusion.33
  47.8 0.6 compare_convert_fusion
  48.5 7.7 %fusion.8 = bf16[1024,2048,1]{1,0,2:T(8,128)(2,1)} fusion(f32[512,1024]{1,0:T(8,128)} %get-tuple-element.30, f32[512,1024]{1,0:T(8,128)} %get-tuple-element.29, f32[512,1024]{1,0:T(8,128)S(1)} %get-tuple-element.28), kind=kLoop, calls=%fused_computation.12 | loop fusion | flops 10485760 | bytes 10485760 | tf_op jit(solution)/shard_map/convert_element_type | solution.py:36
  56.1 0.1 fusion.36
  56.3 0.0 collective-permute-done
  56.3 0.0 collective-permute-done.1
  56.4 0.1 copy.10
  56.5 0.1 copy.8
  56.5 0.2 add_convert_fusion
  56.8 0.2 fusion.23
  57.0 0.0 copy-start
  57.0 3.1 %fusion.37 = f32[4,8,2048]{2,1,0:T(8,128)S(1)} fusion(bf16[4,8,1024]{2,1,0:T(8,128)(2,1)S(1)} %dot_general.22, bf16[1024,2048,1]{1,0,2:T(8,128)(2,1)} %fusion.8), kind=kOutput, calls=%fused_computation.80 | convolution fusion | flops 134217728 | bytes 4521984 | tf_op jit(solution)/shard_map/dot_general | solution.py:84
  60.2 0.3 copy-done
  60.5 0.8 fusion.38
  61.3 3.0 %fusion.39 = f32[4,8,2048]{2,1,0:T(8,128)S(1)} fusion(bf16[4,8,1024]{2,1,0:T(8,128)(2,1)S(1)} %dot_general.26, bf16[1024,2048,1]{1,0,2:T(8,128)(2,1)} %fusion.8), kind=kOutput, calls=%fused_computation.82 | convolution fusion | flops 134217728 | bytes 4521984 | tf_op jit(solution)/shard_map/dot_general | solution.py:84
  64.3 0.1 multiply_reduce_fusion.5
  64.4 0.2 multiply_reduce_fusion.3
  64.6 0.6 add_add_fusion.1
  65.2 0.6 add_add_fusion
  65.8 0.6 add_add_fusion.2
  66.4 0.0 all-reduce.3.cloned.1.call-update
  67.0 31.7 %all-reduce.3.cloned.1.call-done = (f32[8,1024]{1,0:T(8,128)}, f32[8,1024]{1,0:T(8,128)}, f32[8,1024]{1,0:T(8,128)}) async-done(((f32[8,1024]{1,0:T(8,128)}, f32[8,1024]{1,0:T(8,128)}, f32[8,1024]{1,0:T(8,128)}), (f32[8,1024]{1,0:T(8,128)}, f32[8,1024]{1,0:T(8,128)}, f32[8,1024]{1,0:T(8,128)})) %all-reduce.3.cloned.1.call-update) | async-done | bytes 98320 | tf_op jit(solution)/shard_map/psum | solution.py:121
  98.7 0.8 multiply_divide_fusion
  99.5 0.6 reshape.62
  (15 shorter events, 0.3 us)
Async XLA Ops:
  6.5 92.2 %all-reduce.3.cloned.1.call-start = ((), (), s32[]{:S(2)}) async-start(), calls=%async_computation | async-start | bytes 196608 | tf_op jit(solution)/shard_map/psum | solution.py:121
  6.5 18.0 %copy-start.1 = (f32[2,1,12,2048]{3,1,2,0:T(1,128)S(1)}, f32[2,1,12,2048]{3,1,2,0:T(1,128)}, u32[]{:S(2)}) copy-start(f32[2,1,12,2048]{3,1,2,0:T(1,128)} %param.2) | copy-start | bytes 589828
  31.9 15.2 %copy-start.2 = (s32[4]{0:T(128)S(1)}, s32[4]{0:T(128)}, u32[]{:S(2)}) copy-start(s32[4]{0:T(128)} %param.3) | copy-start | bytes 52
  32.2 24.1 %collective-permute-start = (bf16[1,2,12,1024]{3,2,1,0:T(8,128)(2,1)S(1)}, bf16[1,2,12,1024]{3,2,1,0:T(8,128)(2,1)S(1)}, u32[]{:S(2)}, u32[]{:S(2)}) collective-permute-start(bf16[1,2,12,1024]{3,2,1,0:T(8,128)(2,1)S(1)} %broadcast_in_dim_reshape.4), channel_id=1, source_target_pairs={{0,12},{4,0},{8,4},{12,8},{1,13},{5,1},{9,5},{13,9},{2,14},{6,2},{... | collective-permute-start | bytes 147464 | tf_op jit(solution)/shard_map/ppermute | solution.py:15
  37.3 19.0 %collective-permute-start.1 = (bf16[1,2,12,1024]{3,2,1,0:T(8,128)(2,1)S(1)}, bf16[1,2,12,1024]{3,2,1,0:T(8,128)(2,1)S(1)}, u32[]{:S(2)}, u32[]{:S(2)}) collective-permute-start(bf16[1,2,12,1024]{3,2,1,0:T(8,128)(2,1)S(1)} %broadcast_in_dim_reshape.4), channel_id=1, source_target_pairs={{0,8},{4,12},{8,0},{12,4},{1,9},{5,13},{9,1},{13,5},{2,10},{6,14},... | collective-permute-start | bytes 147464 | tf_op jit(solution)/shard_map/ppermute | solution.py:15
  57.0 3.5 %copy-start = (bf16[1024,2048,1]{1,0,2:T(8,128)(2,1)S(1)}, bf16[1024,2048,1]{1,0,2:T(8,128)(2,1)}, u32[]{:S(2)}) copy-start(bf16[1024,2048,1]{1,0,2:T(8,128)(2,1)} %fusion.8) | copy-start | bytes 12582916
Sparse Core Ops, SparseCore 0:
  66.6 32.0 all-reduce.2
where the time goes:
time: 107 us
  other arithmetic  40.8 us (38%)
  waiting for transfers between devices  31.7 us (30%)
  between operations  14.2 us (13%)
  matrix products  13.7 us (13%)
  starting transfers between devices  5.11 us (5%)
  local copies, waits for them, and re-layouts  1.44 us (1%)
    psum x1, waiting for transfers between devices, shards(): linear, cos_sum, sin_sum = lax.psum((linear, cos_sum, sin_sum), 'win')  31.7 us
    cos x1, other arithmetic, forward_table(): return jnp.concatenate([jnp.cos(angles), -jnp.sin(angles)], axis=1)  18 us
    sin x1, other arithmetic, inverse_table(): sine_part = jnp.sin(angles)  9.82 us
    convert_element_type x1, other arithmetic, inverse_table(): return joined.astype(jnp.bfloat16)  7.65 us
    dot_general x3, matrix products, accumulate(): jnp.dot(row_block, backward, preferred_element_type=jnp.float32)  6.91 us
    dot_general x1, matrix products, whiten(): jnp.dot(series, dft_table, precision=lax.Precision.HIGHEST, preferred_ele...  6.83 us
    ppermute x2, starting transfers between devices, passed_along(): lax.ppermute(array, axis, [(i, (i + by) % length) for i in range(length)])  5.1 us
  transfers between devices with their start and end apart: 3, of which 1 were waited for; matrix products, arithmetic and copies ran while one was open for 18% of the time, Pallas kernels for 0%

commit v1 on v0

v1 whole, which is shorter than its diff:
```python
import functools
import math

import jax
import jax.numpy as jnp
import numpy as np
from jax import lax
from jax.experimental import pallas as pl
from jax.experimental.pallas import tpu as pltpu
from jax.sharding import PartitionSpec as P

NFFT = 2048
F = 512
LAGS = 1024
LOWEST = NFFT // 16
LANES = 128

RADIX = 4
PERIOD = NFFT // RADIX
QS = F // RADIX
QUEUE = LOWEST // RADIX + np.arange(QS)

VMEM = pl.BlockSpec(memory_space=pltpu.VMEM)


def split_three(table):
    parts = []
    rest = np.asarray(table, np.float64)
    for _ in range(3):
        part = rest.astype(np.float32).astype(jnp.bfloat16)
        parts.append(part)
        rest = rest - part.astype(np.float64)
    return parts


def forward_tables():
    t0 = np.arange(PERIOD)
    angle = (t0[:, None] * QUEUE[None, :] % PERIOD) * (2 * math.pi / PERIOD)
    cosine, sine = np.cos(angle), np.sin(angle)
    return split_three(np.block([[cosine, -sine], [sine, cosine]]))


def backward_table():
    m = np.arange(PERIOD)
    angle = (QUEUE[:, None] * m[None, :] % PERIOD) * (2 * math.pi / PERIOD)
    cosine, sine = np.cos(angle), np.sin(angle)
    table = np.block([[cosine, sine], [-sine, cosine]]) / math.sqrt(F)
    return table.astype(np.float32).astype(jnp.bfloat16)


def twiddles():
    n = np.arange(PERIOD)
    rows = []
    for r in range(1, RADIX):
        angle = (r * n) * (2 * math.pi / NFFT)
        rows += [np.cos(angle), np.sin(angle)]
    rows += [np.zeros(PERIOD)] * 2
    return np.stack(rows).astype(np.float32)


def whiten_kernel(rows, x_ref, high_ref, mid_ref, low_ref, twiddle_ref, out_ref):
    chunks = PERIOD // LANES
    stride = NFFT // LANES
    real = [[] for _ in range(RADIX)]
    imag = [[] for _ in range(RADIX)]
    for c in range(chunks):
        x0, x1, x2, x3 = (
            x_ref[pl.ds(t1 * chunks + c, rows, stride=stride), :] for t1 in range(RADIX)
        )
        cos1, sin1, cos2, sin2, cos3, sin3 = (
            twiddle_ref[i : i + 1, c * LANES : (c + 1) * LANES] for i in range(6)
        )
        even, odd = x0 + x2, x1 + x3
        a, b = x0 - x2, x1 - x3
        both = even - odd
        real[0].append(even + odd)
        imag[0].append(jnp.zeros_like(even))
        real[1].append(a * cos1 - b * sin1)
        imag[1].append(-(a * sin1 + b * cos1))
        real[2].append(both * cos2)
        imag[2].append(-(both * sin2))
        real[3].append(a * cos3 + b * sin3)
        imag[3].append(b * cos3 - a * sin3)
    series = jnp.concatenate(
        [jnp.concatenate(real[r] + imag[r], axis=1) for r in range(RADIX)], axis=0
    )
    high = series.astype(jnp.bfloat16)
    rest = series - high.astype(jnp.float32)
    mid = rest.astype(jnp.bfloat16)
    low = (rest - mid.astype(jnp.float32)).astype(jnp.bfloat16)
    dot = functools.partial(jnp.dot, preferred_element_type=jnp.float32)
    n = RADIX * rows
    by_high = dot(jnp.concatenate([high, mid, low], axis=0), high_ref[...])
    by_mid = dot(jnp.concatenate([high, mid], axis=0), mid_ref[...])
    by_low = dot(high, low_ref[...])
    small = by_high[2 * n :] + by_mid[n:] + by_low
    spectra = by_high[:n] + ((by_high[n : 2 * n] + by_mid[:n]) + small)
    power = []
    for r in range(RADIX):
        block = spectra[r * rows : (r + 1) * rows]
        power.append(block[:, :QS] * block[:, :QS] + block[:, QS:] * block[:, QS:])
    total = (power[0] + power[1]) + (power[2] + power[3])
    mean = jnp.sum(total, axis=1, keepdims=True) * (1.0 / F)
    floor = 0.09 * (mean + 1e-06)
    for r in range(RADIX):
        block = spectra[r * rows : (r + 1) * rows]
        scale = lax.rsqrt(jnp.maximum(power[r], floor))
        at = 2 * r * QS
        out_ref[:, at : at + QS] = (block[:, :QS] * scale).astype(jnp.bfloat16)
        out_ref[:, at + QS : at + 2 * QS] = (block[:, QS:] * scale).astype(jnp.bfloat16)


def stack_kernel(
    channels,
    segments,
    own_ref,
    first_ref,
    second_ref,
    count_ref,
    table_ref,
    twiddle_ref,
    out_ref,
    own,
    visitor,
    inner,
):
    rows = channels * segments
    pairs = 2 * channels * channels
    own[...] = own_ref[...].astype(jnp.float32)
    visitor[0:rows] = first_ref[...].astype(jnp.float32)
    visitor[rows : 2 * rows] = second_ref[...].astype(jnp.float32)

    place = lax.broadcasted_iota(jnp.int32, (pairs, LANES), 0)
    a_of = place // channels % channels
    sb_of = place // (channels * channels) * channels + place % channels

    def spread(ref, which, choice, count, segment, at):
        value = None
        for i in range(count):
            row = ref[i * segments + segment, pl.ds(at, LANES)]
            row = jnp.broadcast_to(row.reshape(1, LANES), (pairs, LANES))
            value = row if value is None else jnp.where(choice == i, row, value)
        return value

    for r in range(RADIX):
        cross_real, cross_imag = [], []
        at = 2 * r * QS
        for k in range(segments):
            own_re = spread(own, 0, a_of, channels, k, at)
            own_im = spread(own, 0, a_of, channels, k, at + QS)
            vis_re = spread(visitor, 0, sb_of, 2 * channels, k, at)
            vis_im = spread(visitor, 0, sb_of, 2 * channels, k, at + QS)
            cross_real.append(own_re * vis_re + own_im * vis_im)
            cross_imag.append(own_im * vis_re - own_re * vis_im)
        cross = jnp.concatenate(
            [jnp.concatenate(cross_real, axis=0), jnp.concatenate(cross_imag, axis=0)],
            axis=1,
        ).astype(jnp.bfloat16)
        inner[r] = jnp.dot(cross, table_ref[...], preferred_element_type=jnp.float32)

    window = lax.axis_index("win")
    counts = count_ref[...]
    lane = lax.broadcasted_iota(jnp.int32, counts.shape, 1)
    kept_count = jnp.sum(jnp.where(lane == window, counts, 0), axis=1, keepdims=True)
    kept = [
        jnp.broadcast_to((kept_count > k).astype(jnp.float32), (pairs, LANES))
        for k in range(segments)
    ]

    for c in range(PERIOD // LANES):
        low, high = c * LANES, (c + 1) * LANES
        cos1, sin1, cos2, sin2, cos3, sin3 = (
            jnp.broadcast_to(twiddle_ref[i : i + 1, low:high], (pairs, LANES))
            for i in range(6)
        )
        sums = [[None] * 3, [None] * 3]
        for k in range(segments):
            at = slice(k * pairs, (k + 1) * pairs)
            re = [inner[r, at, low:high] for r in range(RADIX)]
            im = [inner[r, at, PERIOD + low : PERIOD + high] for r in range(RADIX)]
            re1, im1 = re[1] * cos1 - im[1] * sin1, re[1] * sin1 + im[1] * cos1
            re2, im2 = re[2] * cos2 - im[2] * sin2, re[2] * sin2 + im[2] * cos2
            re3, im3 = re[3] * cos3 - im[3] * sin3, re[3] * sin3 + im[3] * cos3
            later = (re[0] + re2) + (re1 + re3), (im[0] + im2) + (im1 + im3)
            earlier = (re[0] - re2) + (im1 - im3), (im[0] - im2) - (re1 - re3)
            for half, (direct, quadrature) in enumerate((earlier, later)):
                power = direct * direct + quadrature * quadrature
                scale = lax.rsqrt(jnp.maximum(power, 0.25)) * kept[k]
                terms = (direct * kept[k], direct * scale, quadrature * scale)
                for i, term in enumerate(terms):
                    old = sums[half][i]
                    sums[half][i] = term if old is None else old + term
        for half in range(2):
            for i in range(3):
                out_ref[
                    i * pairs : (i + 1) * pairs,
                    half * PERIOD + low : half * PERIOD + high,
                ] = sums[half][i]


def add_kernel(left_ref, right_ref, out_ref):
    out_ref[...] = left_ref[...] + right_ref[...]


def final_kernel(shape, left_ref, right_ref, count_ref, out_ref):
    total = jnp.sum(count_ref[...], axis=1, keepdims=True).astype(jnp.float32)
    square = total * total
    groups, offsets = shape
    _, _, channels, _, _ = out_ref.shape
    pairs = offsets * channels * channels
    for g in range(groups):
        at = 3 * pairs * g
        linear, cos_sum, sin_sum = (
            left_ref[at + i * pairs : at + (i + 1) * pairs]
            + right_ref[at + i * pairs : at + (i + 1) * pairs]
            for i in range(3)
        )
        result = linear * (cos_sum * cos_sum + sin_sum * sin_sum) / square
        for s in range(offsets):
            for a in range(channels):
                row = (s * channels + a) * channels
                out_ref[0, g * offsets + s, a] = result[row : row + channels]


def call(kernel, out, *args, scratch=(), limit=8 << 20):
    return pl.pallas_call(
        kernel,
        out_shape=out,
        in_specs=[VMEM] * len(args),
        out_specs=VMEM,
        scratch_shapes=list(scratch),
        compiler_params=pltpu.CompilerParams(vmem_limit_bytes=limit),
    )(*args)


def passed_along(array, axis, by):
    length = lax.axis_size(axis)
    return lax.ppermute(array, axis, [(i, (i + by) % length) for i in range(length)])


def shards(traces, seg_count):
    channels, _, segments, _ = traces.shape
    rows = channels * segments
    span_blocks = lax.axis_size("chan") // 2
    windows = lax.axis_size("win")
    twiddle = jnp.asarray(twiddles())

    own = call(
        functools.partial(whiten_kernel, rows),
        jax.ShapeDtypeStruct((rows, 2 * F), jnp.bfloat16),
        traces.reshape(-1, LANES),
        *(jnp.asarray(part) for part in forward_tables()),
        twiddle,
    )

    visitors = [passed_along(own, "chan", -1 - s) for s in range(min(span_blocks, 2))]
    if span_blocks > 2:
        collected = jnp.stack(visitors)
        while collected.shape[0] < span_blocks:
            held = collected.shape[0]
            more = min(held, span_blocks - held)
            arrived = passed_along(collected[:more], "chan", -held)
            collected = jnp.concatenate([collected, arrived], axis=0)
        visitors = [collected[s] for s in range(span_blocks)]

    counts = seg_count.reshape(1, -1)
    backward = jnp.asarray(backward_table())
    pairs = 2 * channels * channels
    stacks = [
        call(
            functools.partial(stack_kernel, channels, segments),
            jax.ShapeDtypeStruct((3 * pairs, LAGS), jnp.float32),
            own,
            visitors[s],
            visitors[s + 1],
            counts,
            backward,
            twiddle,
            scratch=(
                pltpu.VMEM((rows, 2 * F), jnp.float32),
                pltpu.VMEM((2 * rows, 2 * F), jnp.float32),
                pltpu.VMEM((RADIX, segments * pairs, LAGS), jnp.float32),
            ),
        )
        for s in range(0, span_blocks, 2)
    ]
    stack = stacks[0] if len(stacks) == 1 else jnp.concatenate(stacks, axis=0)

    step = 1
    while True:
        arrived = lax.ppermute(stack, "win", [(i, i ^ step) for i in range(windows)])
        step *= 2
        if step == windows:
            break
        stack = call(
            add_kernel, jax.ShapeDtypeStruct(stack.shape, jnp.float32), stack, arrived
        )
    return call(
        functools.partial(final_kernel, (span_blocks // 2, 2)),
        jax.ShapeDtypeStruct((1, span_blocks, channels, channels, LAGS), jnp.float32),
        stack,
        arrived,
        counts,
    )


def solution(mesh):
    placed = (P(("arrays", "chan"), "win", None, None), P("arrays"))
    return jax.shard_map(
        shards,
        mesh=mesh,
        in_specs=placed,
        out_specs=P(("arrays", "chan"), None, None, None, None),
        check_vma=False,
    )
```

time: 107 us -> 21.7 us (0.20)
  other arithmetic: 40.8 us -> 0 us
  waiting for transfers between devices: 31.7 us -> 7.39 us
  between operations: 14.2 us -> 0.05 us
  matrix products: 13.7 us -> 0 us
  local copies, waits for them, and re-layouts: 1.44 us -> 4.78 us
  Pallas kernels: 0 us -> 2.08 us
  starting transfers between devices: 5.11 us -> 7.08 us
    psum x1 -> x0, waiting for transfers between devices: 31.7 us -> none  [shards(): linear, cos_sum, sin_sum = lax.psum((linear, cos_sum, sin_sum), 'win')]
    cos x1 -> x0, other arithmetic: 18 us -> none  [forward_table(): return jnp.concatenate([jnp.cos(angles), -jnp.sin(angles)], axis=1)]
    dot_general x4 -> x0, matrix products: 13.7 us -> none  [the longest x3 6.91 us: accumulate(): jnp.dot(row_block, backward, preferred_element_type=jnp.float32)]
    sin x1 -> x0, other arithmetic: 9.82 us -> none  [inverse_table(): sine_part = jnp.sin(angles)]
    convert_element_type x4 -> x0, other arithmetic: 8.35 us -> none  [the longest x1 7.65 us: inverse_table(): return joined.astype(jnp.bfloat16)]
    ppermute x0 -> x2, waiting for transfers between devices: none -> 4.65 us  [shards(): lax.ppermute(stack, 'win', [(i, i ^ step) for i in range(windows)])]
    unnamed x6 -> x14, local copies, waits for them, and re-layouts: 0.32 us -> 4.78 us
    ppermute x2, waiting for transfers between devices: 0.01 us -> 2.74 us  [passed_along(): lax.ppermute(array, axis, [(i, (i + by) % length) for i in range(length)])]
  transfers between devices with their start and end apart: 3 -> 4, of which waited for: 1 -> 4; matrix products, arithmetic and copies ran while one was open for 18% -> 0% of each run, Pallas kernels for 0% -> 0%
where the time goes in v1:
time: 21.7 us; the launch traced here: 21.4 us
  waiting for transfers between devices  7.39 us (34%)
  starting transfers between devices  7.08 us (33%)
  local copies, waits for them, and re-layouts  4.78 us (22%)
  Pallas kernels  2.08 us (10%)
    ppermute x2, starting transfers between devices, passed_along(): lax.ppermute(array, axis, [(i, (i + by) % length) for i in range(length)])  5.45 us
    unnamed x14, local copies, waits for them, and re-layouts  4.78 us
    ppermute x2, waiting for transfers between devices, shards(): lax.ppermute(stack, 'win', [(i, i ^ step) for i in range(windows)])  4.65 us
    ppermute x2, waiting for transfers between devices, passed_along(): lax.ppermute(array, axis, [(i, (i + by) % length) for i in range(length)])  2.74 us
    pallas_call x4, Pallas kernels, call(): pl.pallas_call(kernel, out_shape=out, in_specs=[VMEM] * len(args), out_sp...  2.08 us
    ppermute x2, starting transfers between devices, shards(): lax.ppermute(stack, 'win', [(i, i ^ step) for i in range(windows)])  1.63 us
  transfers between devices with their start and end apart: 4, of which 4 were waited for; matrix products, arithmetic and copies ran while one was open for 0% of the time, Pallas kernels for 0%

profile of v1, /device:TPU:0, one launch (start us, length us, event | category | flops | bytes accessed | tf_op | source)
XLA Modules:
  0.0 21.4 jit_solution(13951834763014794302)
XLA Ops:
  0.0 0.0 copy-start
  0.0 1.0 %copy-done = bf16[1024,256]{1,0:T(8,128)(2,1)S(1)} copy-done((bf16[1024,256]{1,0:T(8,128)(2,1)S(1)}, bf16[1024,256]{1,0:T(8,128)(2,1)}, u32[]{:S(2)}) %copy-start) | copy-done | bytes 524312
  1.0 0.0 copy-start.1
  1.0 1.0 %copy-done.1 = bf16[1024,256]{1,0:T(8,128)(2,1)S(1)} copy-done((bf16[1024,256]{1,0:T(8,128)(2,1)S(1)}, bf16[1024,256]{1,0:T(8,128)(2,1)}, u32[]{:S(2)}) %copy-start.1) | copy-done | bytes 524312
  2.1 0.0 copy-start.2
  2.1 1.0 %copy-done.2 = bf16[1024,256]{1,0:T(8,128)(2,1)S(1)} copy-done((bf16[1024,256]{1,0:T(8,128)(2,1)S(1)}, bf16[1024,256]{1,0:T(8,128)(2,1)}, u32[]{:S(2)}) %copy-start.2) | copy-done | bytes 524312
  3.1 0.0 copy-start.4
  3.1 0.9 %copy-done.4 = f32[2,1,12,2048]{3,1,2,0:T(1,128)S(1)} copy-done((f32[2,1,12,2048]{3,1,2,0:T(1,128)S(1)}, f32[2,1,12,2048]{3,1,2,0:T(1,128)}, u32[]{:S(2)}) %copy-start.4) | copy-done | bytes 196632
  4.1 0.0 copy-start.5
  4.1 0.7 %copy-done.5 = f32[8,512]{1,0:T(8,128)S(1)} copy-done((f32[8,512]{1,0:T(8,128)S(1)}, f32[8,512]{1,0:T(8,128)}, u32[]{:S(2)}) %copy-start.5) | copy-done | bytes 16408
  4.8 0.0 copy-start.3
  4.8 0.6 %shard_map.73.own_ref = bf16[24,1024]{1,0:T(8,128)(2,1)S(1)} custom-call(f32[384,128]{1,0:T(8,128)S(1)} %bitcast.2, bf16[1024,256]{1,0:T(8,128)(2,1)S(1)} %copy-done.2, bf16[1024,256]{1,0:T(8,128)(2,1)S(1)} %copy-done.1, bf16[1024,256]{1,0:T(8,128)(2,1)S(1)} %copy-done, f32[8,512]{1,0:T(8,128)S(1)} %copy-done.5), custom_call_target="tpu_custom_call" | custom-call | tf_op jit(solution)/shard_map/pallas_call | solution.py:226
  5.4 0.0 copy-start.6
  5.4 4.1 %collective-permute-start.1 = (bf16[24,1024]{1,0:T(8,128)(2,1)S(1)}, bf16[24,1024]{1,0:T(8,128)(2,1)S(1)}, u32[]{:S(2)}, u32[]{:S(2)}) collective-permute-start(bf16[24,1024]{1,0:T(8,128)(2,1)S(1)} %shard_map.73.own_ref), channel_id=1, source_target_pairs={{0,8},{4,12},{8,0},{12,4},{1,9},{5,13},{9,1},{13,5},{2,10},{6,14},... | collective-permute-start | bytes 147464 | tf_op jit(solution)/shard_map/ppermute | solution.py:238
  9.5 1.3 %collective-permute-start = (bf16[24,1024]{1,0:T(8,128)(2,1)S(1)}, bf16[24,1024]{1,0:T(8,128)(2,1)S(1)}, u32[]{:S(2)}, u32[]{:S(2)}) collective-permute-start(bf16[24,1024]{1,0:T(8,128)(2,1)S(1)} %shard_map.73.own_ref), channel_id=1, source_target_pairs={{0,12},{4,0},{8,4},{12,8},{1,13},{5,1},{9,5},{13,9},{2,14},{6,2},{... | collective-permute-start | bytes 147464 | tf_op jit(solution)/shard_map/ppermute | solution.py:238
  10.8 1.4 %collective-permute-done.1.second_ref = bf16[24,1024]{1,0:T(8,128)(2,1)S(1)} collective-permute-done((bf16[24,1024]{1,0:T(8,128)(2,1)S(1)}, bf16[24,1024]{1,0:T(8,128)(2,1)S(1)}, u32[]{:S(2)}, u32[]{:S(2)}) %collective-permute-start.1) | collective-permute-done | bytes 49184 | tf_op jit(solution)/shard_map/ppermute | solution.py:238
  12.2 1.4 %collective-permute-done.first_ref = bf16[24,1024]{1,0:T(8,128)(2,1)S(1)} collective-permute-done((bf16[24,1024]{1,0:T(8,128)(2,1)S(1)}, bf16[24,1024]{1,0:T(8,128)(2,1)S(1)}, u32[]{:S(2)}, u32[]{:S(2)}) %collective-permute-start) | collective-permute-done | bytes 49184 | tf_op jit(solution)/shard_map/ppermute | solution.py:238
  13.6 0.0 copy-done.3
  13.6 0.0 copy-done.6
  13.6 0.8 %shard_map.74.left_ref = f32[24,1024]{1,0:T(8,128)S(1)} custom-call(bf16[24,1024]{1,0:T(8,128)(2,1)S(1)} %shard_map.73.own_ref, bf16[24,1024]{1,0:T(8,128)(2,1)S(1)} %collective-permute-done.first_ref, bf16[24,1024]{1,0:T(8,128)(2,1)S(1)} %collective-permute-done.1.second_ref, s32[1,4]{1,0:T(1,128)S(1)} %bitcast.3, bf16[256,1024]{1,0:T(8,128)(2,1)S(1)} %copy-done.3, ...), custom_call_target="tpu_custom_call" | custom-call | tf_op jit(solution)/shard_map/pallas_call | solution.py:226
  14.4 0.1 collective-permute-start.2
  14.4 1.3 %collective-permute-done.2.right_ref = f32[24,1024]{1,0:T(8,128)S(1)} collective-permute-done((f32[24,1024]{1,0:T(8,128)S(1)}, f32[24,1024]{1,0:T(8,128)S(1)}, u32[]{:S(2)}, u32[]{:S(2)}) %collective-permute-start.2) | collective-permute-done | bytes 98336 | tf_op jit(solution)/shard_map/ppermute | solution.py:291
  15.7 1.6 %collective-permute-start.3 = (f32[24,1024]{1,0:T(8,128)S(1)}, f32[24,1024]{1,0:T(8,128)S(1)}, u32[]{:S(2)}, u32[]{:S(2)}) collective-permute-start(f32[24,1024]{1,0:T(8,128)S(1)} %shard_map.75.left_ref), channel_id=1, source_target_pairs={{0,2},{1,3},{2,0},{3,1},{4,6},{5,7},{6,4},{7,5},{8,10},{9,11},{10,... | collective-permute-start | bytes 294920 | tf_op jit(solution)/shard_map/ppermute | solution.py:291
  17.3 3.4 %collective-permute-done.3.right_ref = f32[24,1024]{1,0:T(8,128)S(1)} collective-permute-done((f32[24,1024]{1,0:T(8,128)S(1)}, f32[24,1024]{1,0:T(8,128)S(1)}, u32[]{:S(2)}, u32[]{:S(2)}) %collective-permute-start.3) | collective-permute-done | bytes 98336 | tf_op jit(solution)/shard_map/ppermute | solution.py:291
  20.7 0.7 %shard_map.76 = f32[1,2,2,2,1024]{4,3,2,1,0:T(2,128)} custom-call(f32[24,1024]{1,0:T(8,128)S(1)} %shard_map.75.left_ref, f32[24,1024]{1,0:T(8,128)S(1)} %collective-permute-done.3.right_ref, s32[1,4]{1,0:T(1,128)S(1)} %bitcast.4), custom_call_target="tpu_custom_call" | custom-call | tf_op jit(solution)/shard_map/pallas_call | solution.py:226
  (1 shorter events, 0.0 us)
Async XLA Ops:
  0.0 1.0 %copy-start = (bf16[1024,256]{1,0:T(8,128)(2,1)S(1)}, bf16[1024,256]{1,0:T(8,128)(2,1)}, u32[]{:S(2)}) copy-start(bf16[1024,256]{1,0:T(8,128)(2,1)} %constant.13.clone.low_ref) | copy-start | bytes 1572868
  1.0 1.0 %copy-start.1 = (bf16[1024,256]{1,0:T(8,128)(2,1)S(1)}, bf16[1024,256]{1,0:T(8,128)(2,1)}, u32[]{:S(2)}) copy-start(bf16[1024,256]{1,0:T(8,128)(2,1)} %constant.12.clone.mid_ref) | copy-start | bytes 1572868
  2.1 1.0 %copy-start.2 = (bf16[1024,256]{1,0:T(8,128)(2,1)S(1)}, bf16[1024,256]{1,0:T(8,128)(2,1)}, u32[]{:S(2)}) copy-start(bf16[1024,256]{1,0:T(8,128)(2,1)} %constant.11.clone.high_ref) | copy-start | bytes 1572868
  3.1 0.9 %copy-start.4 = (f32[2,1,12,2048]{3,1,2,0:T(1,128)S(1)}, f32[2,1,12,2048]{3,1,2,0:T(1,128)}, u32[]{:S(2)}) copy-start(f32[2,1,12,2048]{3,1,2,0:T(1,128)} %param.7) | copy-start | bytes 589828
  4.1 0.7 %copy-start.5 = (f32[8,512]{1,0:T(8,128)S(1)}, f32[8,512]{1,0:T(8,128)}, u32[]{:S(2)}) copy-start(f32[8,512]{1,0:T(8,128)} %constant.10.clone.twiddle_ref) | copy-start | bytes 49156
  4.8 8.8 %copy-start.3 = (bf16[256,1024]{1,0:T(8,128)(2,1)S(1)}, bf16[256,1024]{1,0:T(8,128)(2,1)}, u32[]{:S(2)}) copy-start(bf16[256,1024]{1,0:T(8,128)(2,1)} %constant.14.clone.table_ref) | copy-start | bytes 1572868
  5.4 8.2 %copy-start.6 = (s32[4]{0:T(128)S(1)}, s32[4]{0:T(128)}, u32[]{:S(2)}) copy-start(s32[4]{0:T(128)} %param.8) | copy-start | bytes 52
  5.4 6.8 %collective-permute-start.1 = (bf16[24,1024]{1,0:T(8,128)(2,1)S(1)}, bf16[24,1024]{1,0:T(8,128)(2,1)S(1)}, u32[]{:S(2)}, u32[]{:S(2)}) collective-permute-start(bf16[24,1024]{1,0:T(8,128)(2,1)S(1)} %shard_map.73.own_ref), channel_id=1, source_target_pairs={{0,8},{4,12},{8,0},{12,4},{1,9},{5,13},{9,1},{13,5},{2,10},{6,14},... | collective-permute-start | bytes 147464 | tf_op jit(solution)/shard_map/ppermute | solution.py:238
  9.5 4.1 %collective-permute-start = (bf16[24,1024]{1,0:T(8,128)(2,1)S(1)}, bf16[24,1024]{1,0:T(8,128)(2,1)S(1)}, u32[]{:S(2)}, u32[]{:S(2)}) collective-permute-start(bf16[24,1024]{1,0:T(8,128)(2,1)S(1)} %shard_map.73.own_ref), channel_id=1, source_target_pairs={{0,12},{4,0},{8,4},{12,8},{1,13},{5,1},{9,5},{13,9},{2,14},{6,2},{... | collective-permute-start | bytes 147464 | tf_op jit(solution)/shard_map/ppermute | solution.py:238
  14.4 1.4 %collective-permute-start.2 = (f32[24,1024]{1,0:T(8,128)S(1)}, f32[24,1024]{1,0:T(8,128)S(1)}, u32[]{:S(2)}, u32[]{:S(2)}) collective-permute-start(f32[24,1024]{1,0:T(8,128)S(1)} %shard_map.74.left_ref), channel_id=1, source_target_pairs={{0,1},{1,0},{2,3},{3,2},{4,5},{5,4},{6,7},{7,6},{8,9},{9,8},{10,11... | collective-permute-start | bytes 294920 | tf_op jit(solution)/shard_map/ppermute | solution.py:291
  15.7 4.9 %collective-permute-start.3 = (f32[24,1024]{1,0:T(8,128)S(1)}, f32[24,1024]{1,0:T(8,128)S(1)}, u32[]{:S(2)}, u32[]{:S(2)}) collective-permute-start(f32[24,1024]{1,0:T(8,128)S(1)} %shard_map.75.left_ref), channel_id=1, source_target_pairs={{0,2},{1,3},{2,0},{3,1},{4,6},{5,7},{6,4},{7,5},{8,10},{9,11},{10,... | collective-permute-start | bytes 294920 | tf_op jit(solution)/shard_map/ppermute | solution.py:291

commit v2 on v1

v2 whole, which is shorter than its diff:
```python
import functools
import math

import jax
import jax.numpy as jnp
import numpy as np
from jax import lax
from jax.experimental import pallas as pl
from jax.experimental.pallas import tpu as pltpu
from jax.sharding import PartitionSpec as P

NFFT = 2048
F = 512
LAGS = 1024
LOWEST = NFFT // 16
LANES = 128

RADIX = 4
PERIOD = NFFT // RADIX
QS = F // RADIX
QUEUE = LOWEST // RADIX + np.arange(QS)

VMEM = pl.BlockSpec(memory_space=pltpu.VMEM)
HBM = pl.BlockSpec(memory_space=pltpu.HBM)


def split_three(table):
    parts = []
    rest = np.asarray(table, np.float64)
    for _ in range(3):
        part = rest.astype(np.float32).astype(jnp.bfloat16)
        parts.append(part)
        rest = rest - part.astype(np.float64)
    return parts


def forward_tables():
    t0 = np.arange(PERIOD)
    angle = (t0[:, None] * QUEUE[None, :] % PERIOD) * (2 * math.pi / PERIOD)
    cosine, sine = np.cos(angle), np.sin(angle)
    return split_three(np.block([[cosine, -sine], [sine, cosine]]))


def backward_table():
    m = np.arange(PERIOD)
    angle = (QUEUE[:, None] * m[None, :] % PERIOD) * (2 * math.pi / PERIOD)
    cosine, sine = np.cos(angle), np.sin(angle)
    table = np.block([[cosine, sine], [-sine, cosine]]) / math.sqrt(F)
    return table.astype(np.float32).astype(jnp.bfloat16)


def twiddles():
    n = np.arange(PERIOD)
    rows = []
    for r in range(1, RADIX):
        angle = (r * n) * (2 * math.pi / NFFT)
        rows += [np.cos(angle), np.sin(angle)]
    rows += [np.zeros(PERIOD)] * 2
    return np.stack(rows).astype(np.float32)


def whiten_kernel(
    rows, x_hbm, tables_hbm, twiddle_hbm, out_ref, x_ref, tables, twiddle_ref, sems
):
    copies = [
        pltpu.make_async_copy(x_hbm, x_ref, sems.at[0]),
        pltpu.make_async_copy(twiddle_hbm, twiddle_ref, sems.at[1]),
    ]
    copies += [
        pltpu.make_async_copy(tables_hbm.at[i], tables.at[i], sems.at[2 + i])
        for i in range(3)
    ]
    for copy in copies:
        copy.start()
    copies[0].wait()
    copies[1].wait()

    chunks = PERIOD // LANES
    stride = NFFT // LANES
    real = [[] for _ in range(RADIX)]
    imag = [[] for _ in range(RADIX)]
    for c in range(chunks):
        x0, x1, x2, x3 = (
            x_ref[pl.ds(t1 * chunks + c, rows, stride=stride), :] for t1 in range(RADIX)
        )
        cos1, sin1, cos2, sin2, cos3, sin3 = (
            twiddle_ref[i : i + 1, c * LANES : (c + 1) * LANES] for i in range(6)
        )
        even, odd = x0 + x2, x1 + x3
        a, b = x0 - x2, x1 - x3
        both = even - odd
        real[0].append(even + odd)
        imag[0].append(jnp.zeros_like(even))
        real[1].append(a * cos1 - b * sin1)
        imag[1].append(-(a * sin1 + b * cos1))
        real[2].append(both * cos2)
        imag[2].append(-(both * sin2))
        real[3].append(a * cos3 + b * sin3)
        imag[3].append(b * cos3 - a * sin3)
    series = jnp.concatenate(
        [jnp.concatenate(real[r] + imag[r], axis=1) for r in range(RADIX)], axis=0
    )
    high = series.astype(jnp.bfloat16)
    rest = series - high.astype(jnp.float32)
    mid = rest.astype(jnp.bfloat16)
    low = (rest - mid.astype(jnp.float32)).astype(jnp.bfloat16)
    dot = functools.partial(jnp.dot, preferred_element_type=jnp.float32)
    n = RADIX * rows
    copies[2].wait()
    by_high = dot(jnp.concatenate([high, mid, low], axis=0), tables[0])
    copies[3].wait()
    by_mid = dot(jnp.concatenate([high, mid], axis=0), tables[1])
    copies[4].wait()
    by_low = dot(high, tables[2])
    small = by_high[2 * n :] + by_mid[n:] + by_low
    spectra = by_high[:n] + ((by_high[n : 2 * n] + by_mid[:n]) + small)
    power = []
    for r in range(RADIX):
        block = spectra[r * rows : (r + 1) * rows]
        power.append(block[:, :QS] * block[:, :QS] + block[:, QS:] * block[:, QS:])
    total = (power[0] + power[1]) + (power[2] + power[3])
    mean = jnp.sum(total, axis=1, keepdims=True) * (1.0 / F)
    floor = 0.09 * (mean + 1e-06)
    for r in range(RADIX):
        block = spectra[r * rows : (r + 1) * rows]
        scale = lax.rsqrt(jnp.maximum(power[r], floor))
        at = 2 * r * QS
        out_ref[:, at : at + QS] = (block[:, :QS] * scale).astype(jnp.bfloat16)
        out_ref[:, at + QS : at + 2 * QS] = (block[:, QS:] * scale).astype(jnp.bfloat16)


def stack_kernel(
    channels,
    segments,
    own_ref,
    own_mate_ref,
    visitor_ref,
    visitor_mate_ref,
    count_ref,
    table_ref,
    twiddle_ref,
    out_ref,
    own,
    visitor,
    inner,
):
    rows = channels * segments
    pairs = channels * channels
    group = 2 * pairs
    own[0:rows] = own_ref[...].astype(jnp.float32)
    own[rows : 2 * rows] = own_mate_ref[...].astype(jnp.float32)
    visitor[0:rows] = visitor_ref[...].astype(jnp.float32)
    visitor[rows : 2 * rows] = visitor_mate_ref[...].astype(jnp.float32)

    place = lax.broadcasted_iota(jnp.int32, (group, LANES), 0)
    own_of = place // channels
    visitor_of = place // pairs * channels + place % channels
    is_own = place < pairs

    def spread(ref, choice, segment, at):
        value = None
        for i in range(2 * channels):
            row = ref[pl.ds(i * segments + segment, 1), pl.ds(at, LANES)]
            row = jnp.broadcast_to(row, (group, LANES))
            value = row if value is None else jnp.where(choice == i, row, value)
        return value

    for r in range(RADIX):
        cross_real, cross_imag = [], []
        at = 2 * r * QS
        for k in range(segments):
            own_re = spread(own, own_of, k, at)
            own_im = spread(own, own_of, k, at + QS)
            vis_re = spread(visitor, visitor_of, k, at)
            vis_im = spread(visitor, visitor_of, k, at + QS)
            cross_real.append(own_re * vis_re + own_im * vis_im)
            cross_imag.append(own_im * vis_re - own_re * vis_im)
        cross = jnp.concatenate(
            [jnp.concatenate(cross_real, axis=0), jnp.concatenate(cross_imag, axis=0)],
            axis=1,
        ).astype(jnp.bfloat16)
        inner[r] = jnp.dot(cross, table_ref[...], preferred_element_type=jnp.float32)

    window = lax.axis_index("win")
    mate = window + 1 - 2 * (window % 2)
    counts = count_ref[...]
    lane = lax.broadcasted_iota(jnp.int32, counts.shape, 1)
    kept_own, kept_mate = (
        jnp.sum(jnp.where(lane == w, counts, 0), axis=1, keepdims=True)
        for w in (window, mate)
    )
    kept_count = jnp.where(is_own, kept_own, kept_mate)
    kept = [(kept_count > k).astype(jnp.float32) for k in range(segments)]

    for c in range(PERIOD // LANES):
        low, high = c * LANES, (c + 1) * LANES
        cos1, sin1, cos2, sin2, cos3, sin3 = (
            jnp.broadcast_to(twiddle_ref[i : i + 1, low:high], (group, LANES))
            for i in range(6)
        )
        sums = [[None] * 3, [None] * 3]
        for k in range(segments):
            at = slice(k * group, (k + 1) * group)
            re = [inner[r, at, low:high] for r in range(RADIX)]
            im = [inner[r, at, PERIOD + low : PERIOD + high] for r in range(RADIX)]
            re1, im1 = re[1] * cos1 - im[1] * sin1, re[1] * sin1 + im[1] * cos1
            re2, im2 = re[2] * cos2 - im[2] * sin2, re[2] * sin2 + im[2] * cos2
            re3, im3 = re[3] * cos3 - im[3] * sin3, re[3] * sin3 + im[3] * cos3
            later = (re[0] + re2) + (re1 + re3), (im[0] + im2) + (im1 + im3)
            earlier = (re[0] - re2) + (im1 - im3), (im[0] - im2) - (re1 - re3)
            for half, (direct, quadrature) in enumerate((earlier, later)):
                power = direct * direct + quadrature * quadrature
                scale = lax.rsqrt(jnp.maximum(power, 0.25)) * kept[k]
                terms = (direct * kept[k], direct * scale, quadrature * scale)
                for i, term in enumerate(terms):
                    old = sums[half][i]
                    sums[half][i] = term if old is None else old + term
        for i in range(3):
            first, second = (
                sums[half][i] + pltpu.roll(sums[half][i], pairs, axis=0)
                for half in range(2)
            )
            out_ref[i * group : (i + 1) * group, low:high] = jnp.where(
                is_own, first, second
            )


def add_kernel(left_ref, right_ref, out_ref):
    out_ref[...] = left_ref[...] + right_ref[...]


def result_kernel(left_ref, right_ref, count_ref, out_ref):
    total = jnp.sum(count_ref[...], axis=1, keepdims=True).astype(jnp.float32)
    square = total * total
    group = out_ref.shape[1]
    for offset in range(out_ref.shape[0]):
        linear, cos_sum, sin_sum = (
            left_ref[offset, i * group : (i + 1) * group]
            + right_ref[offset, i * group : (i + 1) * group]
            for i in range(3)
        )
        out_ref[offset] = linear * (cos_sum * cos_sum + sin_sum * sin_sum) / square


def join_kernel(own_ref, mate_ref, out_ref):
    core = lax.axis_index("win") % 2
    channels = out_ref.shape[2]
    half_lags = own_ref.shape[2]
    for ref, parity in ((own_ref, core), (mate_ref, 1 - core)):
        for offset in range(own_ref.shape[0]):
            for half in range(2):
                for a in range(channels):
                    row = (half * channels + a) * channels
                    lags = slice(half * half_lags, (half + 1) * half_lags)
                    out_ref[0, 2 * offset + parity, a, :, lags] = ref[
                        offset, row : row + channels
                    ]


def call(kernel, out, *args, specs=None, scratch=(), limit=8 << 20):
    return pl.pallas_call(
        kernel,
        out_shape=out,
        in_specs=[VMEM] * len(args) if specs is None else specs,
        out_specs=VMEM,
        scratch_shapes=list(scratch),
        compiler_params=pltpu.CompilerParams(vmem_limit_bytes=limit),
    )(*args)


def shards(traces, seg_count):
    channels, _, segments, _ = traces.shape
    rows = channels * segments
    blocks = lax.axis_size("chan")
    windows = lax.axis_size("win")
    offsets = blocks // 4
    pairs = channels * channels
    group = 2 * pairs
    twiddle = jnp.asarray(twiddles())
    tables = jnp.asarray(np.stack(forward_tables()))
    series = traces.reshape(-1, LANES)

    own = call(
        functools.partial(whiten_kernel, rows),
        jax.ShapeDtypeStruct((rows, 2 * F), jnp.bfloat16),
        *(pltpu.with_memory_space_constraint(x, pltpu.HBM) for x in (series, tables, twiddle)),
        specs=[HBM] * 3,
        scratch=(
            pltpu.VMEM(series.shape, jnp.float32),
            pltpu.VMEM(tables.shape, jnp.bfloat16),
            pltpu.VMEM(twiddle.shape, jnp.float32),
            pltpu.SemaphoreType.DMA((5,)),
        ),
    )

    def to_mate(array):
        return lax.ppermute(array, "win", [(w, w ^ 1) for w in range(windows)])

    def from_block(array, offset, flip):
        moves = []
        for z in range(blocks):
            for w in range(windows):
                source = (z + offset + w % 2) % blocks * windows + (w ^ flip)
                moves.append((source, z * windows + w))
        return lax.ppermute(array, ("chan", "win"), moves)

    counts = seg_count.reshape(1, -1)
    backward = jnp.asarray(backward_table())
    own_mate = to_mate(own)
    stacks = []
    for j in range(offsets):
        visitor = from_block(own, 1 + 2 * j, 0)
        visitor_mate = from_block(own, 1 + 2 * j, 1)
        stacks.append(
            call(
                functools.partial(stack_kernel, channels, segments),
                jax.ShapeDtypeStruct((3 * group, PERIOD), jnp.float32),
                own,
                own_mate,
                visitor,
                visitor_mate,
                counts,
                backward,
                twiddle,
                scratch=(
                    pltpu.VMEM((2 * rows, 2 * F), jnp.float32),
                    pltpu.VMEM((2 * rows, 2 * F), jnp.float32),
                    pltpu.VMEM((RADIX, segments * group, 2 * PERIOD), jnp.float32),
                ),
            )
        )
    stack = jnp.stack(stacks)

    step = 2
    while True:
        arrived = lax.ppermute(stack, "win", [(w, w ^ step) for w in range(windows)])
        step *= 2
        if step == windows:
            break
        stack = call(
            add_kernel, jax.ShapeDtypeStruct(stack.shape, jnp.float32), stack, arrived
        )
    result = call(
        result_kernel,
        jax.ShapeDtypeStruct((offsets, group, PERIOD), jnp.float32),
        stack,
        arrived,
        counts,
    )
    return call(
        join_kernel,
        jax.ShapeDtypeStruct((1, 2 * offsets, channels, channels, LAGS), jnp.float32),
        result,
        to_mate(result),
    )


def solution(mesh):
    placed = (P(("arrays", "chan"), "win", None, None), P("arrays"))
    return jax.shard_map(
        shards,
        mesh=mesh,
        in_specs=placed,
        out_specs=P(("arrays", "chan"), None, None, None, None),
        check_vma=False,
    )
```

time: 21.7 us -> 17.1 us (0.79)
  local copies, waits for them, and re-layouts: 4.78 us -> 0.01 us
  Pallas kernels: 2.08 us -> 3.89 us
  waiting for transfers between devices: 7.39 us -> 5.84 us
    unnamed x14 -> x6, local copies, waits for them, and re-layouts: 4.78 us -> 0.01 us
    pallas_call x4, Pallas kernels: 2.08 us -> 3.89 us  [call(): pl.pallas_call(kernel, out_shape=out, in_specs=[VMEM] * len(args) if spec...]
    ppermute x4 -> x5, waiting for transfers between devices: 7.39 us -> 5.84 us  [the longest x1 2.6 us: shards(): lax.ppermute(stack, 'win', [(w, w ^ step) for w in range(windows)])]
    ppermute x4 -> x5, starting transfers between devices: 7.08 us -> 7.18 us  [the longest x2 5.17 us: from_block(): return lax.ppermute(array, ('chan', 'win'), moves)]
  transfers between devices with their start and end apart: 4 -> 5, of which waited for: 4 -> 4; matrix products, arithmetic and copies ran while one was open for 0% -> 0% of each run, Pallas kernels for 0% -> 0%
where the time goes in v2:
time: 17.1 us; the launch traced here: 17 us
  starting transfers between devices  7.18 us (42%)
  waiting for transfers between devices  5.84 us (34%)
  Pallas kernels  3.89 us (23%)
    ppermute x2, starting transfers between devices, from_block(): return lax.ppermute(array, ('chan', 'win'), moves)  5.17 us
    pallas_call x4, Pallas kernels, call(): pl.pallas_call(kernel, out_shape=out, in_specs=[VMEM] * len(args) if spec...  3.89 us
    ppermute x1, waiting for transfers between devices, shards(): lax.ppermute(stack, 'win', [(w, w ^ step) for w in range(windows)])  2.6 us
    ppermute x2, waiting for transfers between devices, from_block(): return lax.ppermute(array, ('chan', 'win'), moves)  2.4 us
    ppermute x1, starting transfers between devices, shards(): lax.ppermute(stack, 'win', [(w, w ^ step) for w in range(windows)])  1.56 us
    ppermute x2, waiting for transfers between devices, to_mate(): return lax.ppermute(array, 'win', [(w, w ^ 1) for w in range(windows)])  0.84 us
    ppermute x2, starting transfers between devices, to_mate(): return lax.ppermute(array, 'win', [(w, w ^ 1) for w in range(windows)])  0.46 us
  transfers between devices with their start and end apart: 5, of which 4 were waited for; matrix products, arithmetic and copies ran while one was open for 0% of the time, Pallas kernels for 0%

profile of v2, /device:TPU:0, one launch (start us, length us, event | category | flops | bytes accessed | tf_op | source)
XLA Modules:
  0.0 17.0 jit_solution(9362627187685280742)
XLA Ops:
  0.0 0.0 copy-start.1
  0.0 0.0 copy-start
  0.0 0.0 copy-start.2
  0.0 2.3 %shard_map.55.own_ref = bf16[24,1024]{1,0:T(8,128)(2,1)S(1)} custom-call(f32[384,128]{1,0:T(8,128)} %bitcast.7, bf16[3,1024,256]{2,1,0:T(8,128)(2,1)} %constant.7.clone.tables_hbm, f32[8,512]{1,0:T(8,128)} %constant.6.clone.twiddle_hbm.twiddle_ref), custom_call_target="tpu_custom_call" | custom-call | tf_op jit(solution)/shard_map/pallas_call | solution.py:261
  2.3 3.5 %collective-permute-start.2 = (bf16[24,1024]{1,0:T(8,128)(2,1)S(1)}, bf16[24,1024]{1,0:T(8,128)(2,1)S(1)}, u32[]{:S(2)}, u32[]{:S(2)}) collective-permute-start(bf16[24,1024]{1,0:T(8,128)(2,1)S(1)} %shard_map.55.own_ref), channel_id=1, source_target_pairs={{5,0},{8,1},{7,2},{10,3},{9,4},{12,5},{11,6},{14,7},{13,8},{0,9},{... | collective-permute-start | bytes 147464 | tf_op jit(solution)/shard_map/ppermute | solution.py:305
  5.9 1.6 %collective-permute-start.1 = (bf16[24,1024]{1,0:T(8,128)(2,1)S(1)}, bf16[24,1024]{1,0:T(8,128)(2,1)S(1)}, u32[]{:S(2)}, u32[]{:S(2)}) collective-permute-start(bf16[24,1024]{1,0:T(8,128)(2,1)S(1)} %shard_map.55.own_ref), channel_id=1, source_target_pairs={{4,0},{9,1},{6,2},{11,3},{8,4},{13,5},{10,6},{15,7},{12,8},{1,9},{... | collective-permute-start | bytes 147464 | tf_op jit(solution)/shard_map/ppermute | solution.py:305
  7.5 0.1 collective-permute-start
  7.6 0.1 collective-permute-done.2.visitor_mate_ref
  7.6 2.3 %collective-permute-done.1.visitor_ref = bf16[24,1024]{1,0:T(8,128)(2,1)S(1)} collective-permute-done((bf16[24,1024]{1,0:T(8,128)(2,1)S(1)}, bf16[24,1024]{1,0:T(8,128)(2,1)S(1)}, u32[]{:S(2)}, u32[]{:S(2)}) %collective-permute-start.1) | collective-permute-done | bytes 49184 | tf_op jit(solution)/shard_map/ppermute | solution.py:305
  10.0 0.0 collective-permute-done.own_mate_ref
  10.0 0.0 copy-done.1
  10.0 0.0 copy-done
  10.0 0.0 copy-done.2
  10.0 0.9 %shard_map.56 = f32[24,512]{1,0:T(8,128)S(1)} custom-call(bf16[24,1024]{1,0:T(8,128)(2,1)S(1)} %shard_map.55.own_ref, bf16[24,1024]{1,0:T(8,128)(2,1)S(1)} %collective-permute-done.own_mate_ref, bf16[24,1024]{1,0:T(8,128)(2,1)S(1)} %collective-permute-done.1.visitor_ref, bf16[24,1024]{1,0:T(8,128)(2,1)S(1)} %collective-permute-done.2.visitor_mate_ref, ...), custom_call_target="tpu_custom_call" | custom-call | tf_op jit(solution)/shard_map/pallas_call | solution.py:261
  10.8 1.6 %collective-permute-start.3 = (f32[1,24,512]{2,1,0:T(8,128)S(1)}, f32[1,24,512]{2,1,0:T(8,128)S(1)}, u32[]{:S(2)}, u32[]{:S(2)}) collective-permute-start(f32[1,24,512]{2,1,0:T(8,128)S(1)} %bitcast.3), channel_id=1, source_target_pairs={{0,2},{1,3},{2,0},{3,1},{4,6},{5,7},{6,4},{7,5},{8,10},{9,11},{10,... | collective-permute-start | bytes 147464 | tf_op jit(solution)/shard_map/ppermute | solution.py:336
  12.4 2.6 %collective-permute-done.3.right_ref = f32[1,24,512]{2,1,0:T(8,128)S(1)} collective-permute-done((f32[1,24,512]{2,1,0:T(8,128)S(1)}, f32[1,24,512]{2,1,0:T(8,128)S(1)}, u32[]{:S(2)}, u32[]{:S(2)}) %collective-permute-start.3) | collective-permute-done | bytes 49184 | tf_op jit(solution)/shard_map/ppermute | solution.py:336
  15.0 0.1 shard_map.57.own_ref
  15.1 0.4 %collective-permute-start.4 = (f32[1,8,512]{2,1,0:T(8,128)S(1)}, f32[1,8,512]{2,1,0:T(8,128)S(1)}, u32[]{:S(2)}, u32[]{:S(2)}) collective-permute-start(f32[1,8,512]{2,1,0:T(8,128)S(1)} %shard_map.57.own_ref), channel_id=1, source_target_pairs={{0,1},{1,0},{2,3},{3,2},{4,5},{5,4},{6,7},{7,6},{8,9},{9,8},{10,11... | collective-permute-start | bytes 49160 | tf_op jit(solution)/shard_map/ppermute | solution.py:297
  15.5 0.8 %collective-permute-done.4.mate_ref = f32[1,8,512]{2,1,0:T(8,128)S(1)} collective-permute-done((f32[1,8,512]{2,1,0:T(8,128)S(1)}, f32[1,8,512]{2,1,0:T(8,128)S(1)}, u32[]{:S(2)}, u32[]{:S(2)}) %collective-permute-start.4) | collective-permute-done | bytes 16416 | tf_op jit(solution)/shard_map/ppermute | solution.py:297
  16.3 0.6 %shard_map.58 = f32[1,2,2,2,1024]{4,3,2,1,0:T(2,128)} custom-call(f32[1,8,512]{2,1,0:T(8,128)S(1)} %shard_map.57.own_ref, f32[1,8,512]{2,1,0:T(8,128)S(1)} %collective-permute-done.4.mate_ref), custom_call_target="tpu_custom_call" | custom-call | tf_op jit(solution)/shard_map/pallas_call | solution.py:261
Async XLA Ops:
  0.0 10.0 %copy-start.1 = (f32[8,512]{1,0:T(8,128)S(1)}, f32[8,512]{1,0:T(8,128)}, u32[]{:S(2)}) copy-start(f32[8,512]{1,0:T(8,128)} %constant.6.clone.twiddle_hbm.twiddle_ref) | copy-start | bytes 49156
  0.0 10.0 %copy-start = (bf16[256,1024]{1,0:T(8,128)(2,1)S(1)}, bf16[256,1024]{1,0:T(8,128)(2,1)}, u32[]{:S(2)}) copy-start(bf16[256,1024]{1,0:T(8,128)(2,1)} %constant.8.clone.table_ref) | copy-start | bytes 1572868
  0.0 10.0 %copy-start.2 = (s32[4]{0:T(128)S(1)}, s32[4]{0:T(128)}, u32[]{:S(2)}) copy-start(s32[4]{0:T(128)} %param.6) | copy-start | bytes 52
  2.3 5.3 %collective-permute-start.2 = (bf16[24,1024]{1,0:T(8,128)(2,1)S(1)}, bf16[24,1024]{1,0:T(8,128)(2,1)S(1)}, u32[]{:S(2)}, u32[]{:S(2)}) collective-permute-start(bf16[24,1024]{1,0:T(8,128)(2,1)S(1)} %shard_map.55.own_ref), channel_id=1, source_target_pairs={{5,0},{8,1},{7,2},{10,3},{9,4},{12,5},{11,6},{14,7},{13,8},{0,9},{... | collective-permute-start | bytes 147464 | tf_op jit(solution)/shard_map/ppermute | solution.py:305
  5.9 4.1 %collective-permute-start.1 = (bf16[24,1024]{1,0:T(8,128)(2,1)S(1)}, bf16[24,1024]{1,0:T(8,128)(2,1)S(1)}, u32[]{:S(2)}, u32[]{:S(2)}) collective-permute-start(bf16[24,1024]{1,0:T(8,128)(2,1)S(1)} %shard_map.55.own_ref), channel_id=1, source_target_pairs={{4,0},{9,1},{6,2},{11,3},{8,4},{13,5},{10,6},{15,7},{12,8},{1,9},{... | collective-permute-start | bytes 147464 | tf_op jit(solution)/shard_map/ppermute | solution.py:305
  7.5 2.5 %collective-permute-start = (bf16[24,1024]{1,0:T(8,128)(2,1)S(1)}, bf16[24,1024]{1,0:T(8,128)(2,1)S(1)}, u32[]{:S(2)}, u32[]{:S(2)}) collective-permute-start(bf16[24,1024]{1,0:T(8,128)(2,1)S(1)} %shard_map.55.own_ref), channel_id=1, source_target_pairs={{0,1},{1,0},{2,3},{3,2},{4,5},{5,4},{6,7},{7,6},{8,9},{9,8},{10,11... | collective-permute-start | bytes 147464 | tf_op jit(solution)/shard_map/ppermute | solution.py:297
  10.8 4.2 %collective-permute-start.3 = (f32[1,24,512]{2,1,0:T(8,128)S(1)}, f32[1,24,512]{2,1,0:T(8,128)S(1)}, u32[]{:S(2)}, u32[]{:S(2)}) collective-permute-start(f32[1,24,512]{2,1,0:T(8,128)S(1)} %bitcast.3), channel_id=1, source_target_pairs={{0,2},{1,3},{2,0},{3,1},{4,6},{5,7},{6,4},{7,5},{8,10},{9,11},{10,... | collective-permute-start | bytes 147464 | tf_op jit(solution)/shard_map/ppermute | solution.py:336
  15.1 1.2 %collective-permute-start.4 = (f32[1,8,512]{2,1,0:T(8,128)S(1)}, f32[1,8,512]{2,1,0:T(8,128)S(1)}, u32[]{:S(2)}, u32[]{:S(2)}) collective-permute-start(f32[1,8,512]{2,1,0:T(8,128)S(1)} %shard_map.57.own_ref), channel_id=1, source_target_pairs={{0,1},{1,0},{2,3},{3,2},{4,5},{5,4},{6,7},{7,6},{8,9},{9,8},{10,11... | collective-permute-start | bytes 49160 | tf_op jit(solution)/shard_map/ppermute | solution.py:297

commit v3 on v2

--- a/solution.py
+++ b/solution.py
@@ -18,7 +18,11 @@
 RADIX = 4
 PERIOD = NFFT // RADIX
 QS = F // RADIX
-QUEUE = LOWEST // RADIX + np.arange(QS)
+SPLIT = 8
+SPAN = NFFT // SPLIT
+NARROW = F // SPLIT
+FORWARD_Q = LOWEST // SPLIT + np.arange(NARROW)
+BACKWARD_Q = np.concatenate([2 * FORWARD_Q, 2 * FORWARD_Q + 1])
 
 VMEM = pl.BlockSpec(memory_space=pltpu.VMEM)
 HBM = pl.BlockSpec(memory_space=pltpu.HBM)
@@ -35,28 +39,48 @@
 
 
 def forward_tables():
-    t0 = np.arange(PERIOD)
-    angle = (t0[:, None] * QUEUE[None, :] % PERIOD) * (2 * math.pi / PERIOD)
+    t0 = np.arange(SPAN)
+    angle = (t0[:, None] * FORWARD_Q[None, :] % SPAN) * (2 * math.pi / SPAN)
     cosine, sine = np.cos(angle), np.sin(angle)
     return split_three(np.block([[cosine, -sine], [sine, cosine]]))
 
 
 def backward_table():
     m = np.arange(PERIOD)
-    angle = (QUEUE[:, None] * m[None, :] % PERIOD) * (2 * math.pi / PERIOD)
-    cosine, sine = np.cos(angle), np.sin(angle)
-    table = np.block([[cosine, sine], [-sine, cosine]]) / math.sqrt(F)
+    angle = (BACKWARD_Q[:, None] * m[None, :] % PERIOD) * (2 * math.pi / PERIOD)
+    table = np.block([np.cos(angle), np.sin(angle)]) / math.sqrt(F)
     return table.astype(np.float32).astype(jnp.bfloat16)
 
 
-def twiddles():
-    n = np.arange(PERIOD)
+def twiddles(count, length):
+    n = np.arange(length)
     rows = []
-    for r in range(1, RADIX):
+    for r in range(1, count):
         angle = (r * n) * (2 * math.pi / NFFT)
         rows += [np.cos(angle), np.sin(angle)]
-    rows += [np.zeros(PERIOD)] * 2
+    rows += [np.zeros(length)] * 2
     return np.stack(rows).astype(np.float32)
+
+
+def eight_points(x):
+    half = math.sqrt(0.5)
+    s04, d04, s26, d26 = x[0] + x[4], x[0] - x[4], x[2] + x[6], x[2] - x[6]
+    s15, d15, s37, d37 = x[1] + x[5], x[1] - x[5], x[3] + x[7], x[3] - x[7]
+    even, odd = s04 + s26, s15 + s37
+    plus, minus = (d15 + d37) * half, (d15 - d37) * half
+    two = s04 - s26, s37 - s15
+    one = d04 + minus, -(d26 + plus)
+    three = d04 - minus, d26 - plus
+    return [
+        (even + odd, None),
+        one,
+        two,
+        three,
+        (even - odd, None),
+        (three[0], -three[1]),
+        (two[0], -two[1]),
+        (one[0], -one[1]),
+    ]
 
 
 def whiten_kernel(
@@ -72,61 +96,62 @@
     ]
     for copy in copies:
         copy.start()
-    copies[0].wait()
-    copies[1].wait()
-
-    chunks = PERIOD // LANES
-    stride = NFFT // LANES
-    real = [[] for _ in range(RADIX)]
-    imag = [[] for _ in range(RADIX)]
+    for copy in copies:
+        copy.wait()
+
+    chunks = SPAN // LANES
+    real = [[] for _ in range(SPLIT)]
+    imag = [[] for _ in range(SPLIT)]
     for c in range(chunks):
-        x0, x1, x2, x3 = (
-            x_ref[pl.ds(t1 * chunks + c, rows, stride=stride), :] for t1 in range(RADIX)
-        )
-        cos1, sin1, cos2, sin2, cos3, sin3 = (
-            twiddle_ref[i : i + 1, c * LANES : (c + 1) * LANES] for i in range(6)
-        )
-        even, odd = x0 + x2, x1 + x3
-        a, b = x0 - x2, x1 - x3
-        both = even - odd
-        real[0].append(even + odd)
-        imag[0].append(jnp.zeros_like(even))
-        real[1].append(a * cos1 - b * sin1)
-        imag[1].append(-(a * sin1 + b * cos1))
-        real[2].append(both * cos2)
-        imag[2].append(-(both * sin2))
-        real[3].append(a * cos3 + b * sin3)
-        imag[3].append(b * cos3 - a * sin3)
+        x = [
+            x_ref[pl.ds(t1 * chunks + c, rows, stride=SPLIT * chunks), :]
+            for t1 in range(SPLIT)
+        ]
+        for r, (re, im) in enumerate(eight_points(x)):
+            if r > 0:
+                cosine, sine = (
+                    twiddle_ref[2 * r - 2 + i, c * LANES : (c + 1) * LANES].reshape(1, LANES)
+                    for i in range(2)
+                )
+                if im is None:
+                    re, im = re * cosine, -(re * sine)
+                else:
+                    re, im = re * cosine + im * sine, im * cosine - re * sine
+            real[r].append(re)
+            imag[r].append(jnp.zeros_like(re) if im is None else im)
     series = jnp.concatenate(
-        [jnp.concatenate(real[r] + imag[r], axis=1) for r in range(RADIX)], axis=0
+        [jnp.concatenate(real[r] + imag[r], axis=1) for r in range(SPLIT)], axis=0
     )
     high = series.astype(jnp.bfloat16)
     rest = series - high.astype(jnp.float32)
     mid = rest.astype(jnp.bfloat16)
     low = (rest - mid.astype(jnp.float32)).astype(jnp.bfloat16)
     dot = functools.partial(jnp.dot, preferred_element_type=jnp.float32)
-    n = RADIX * rows
-    copies[2].wait()
+    n = SPLIT * rows
     by_high = dot(jnp.concatenate([high, mid, low], axis=0), tables[0])
-    copies[3].wait()
     by_mid = dot(jnp.concatenate([high, mid], axis=0), tables[1])
-    copies[4].wait()
     by_low = dot(high, tables[2])
     small = by_high[2 * n :] + by_mid[n:] + by_low
     spectra = by_high[:n] + ((by_high[n : 2 * n] + by_mid[:n]) + small)
+    blocks = [spectra[r * rows : (r + 1) * rows] for r in range(SPLIT)]
     power = []
+    for block in blocks:
+        square = block * block
+        power.append(square + pltpu.roll(square, NARROW, axis=1))
+    total = ((power[0] + power[1]) + (power[2] + power[3])) + (
+        (power[4] + power[5]) + (power[6] + power[7])
+    )
+    mean = jnp.sum(total, axis=1, keepdims=True) * (0.5 / F)
+    floor = 0.09 * (mean + 1e-06)
+    left = lax.broadcasted_iota(jnp.int32, (rows, LANES), 1) < NARROW
+    white = [b * lax.rsqrt(jnp.maximum(p, floor)) for b, p in zip(blocks, power)]
     for r in range(RADIX):
-        block = spectra[r * rows : (r + 1) * rows]
-        power.append(block[:, :QS] * block[:, :QS] + block[:, QS:] * block[:, QS:])
-    total = (power[0] + power[1]) + (power[2] + power[3])
-    mean = jnp.sum(total, axis=1, keepdims=True) * (1.0 / F)
-    floor = 0.09 * (mean + 1e-06)
-    for r in range(RADIX):
-        block = spectra[r * rows : (r + 1) * rows]
-        scale = lax.rsqrt(jnp.maximum(power[r], floor))
+        first, second = white[r], white[r + RADIX]
         at = 2 * r * QS
-        out_ref[:, at : at + QS] = (block[:, :QS] * scale).astype(jnp.bfloat16)
-        out_ref[:, at + QS : at + 2 * QS] = (block[:, QS:] * scale).astype(jnp.bfloat16)
+        re = jnp.where(left, first, pltpu.roll(second, NARROW, axis=1))
+        im = jnp.where(left, pltpu.roll(first, NARROW, axis=1), second)
+        out_ref[:, at : at + QS] = re.astype(jnp.bfloat16)
+        out_ref[:, at + QS : at + 2 * QS] = im.astype(jnp.bfloat16)
 
 
 def stack_kernel(
@@ -142,6 +167,7 @@
     out_ref,
     own,
     visitor,
+    table,
     inner,
 ):
     rows = channels * segments
@@ -151,6 +177,10 @@
     own[rows : 2 * rows] = own_mate_ref[...].astype(jnp.float32)
     visitor[0:rows] = visitor_ref[...].astype(jnp.float32)
     visitor[rows : 2 * rows] = visitor_mate_ref[...].astype(jnp.float32)
+
+    table[0:QS] = table_ref[...]
+    table[QS : 2 * QS, 0:PERIOD] = -table_ref[:, PERIOD:]
+    table[QS : 2 * QS, PERIOD:] = table_ref[:, 0:PERIOD]
 
     place = lax.broadcasted_iota(jnp.int32, (group, LANES), 0)
     own_of = place // channels
@@ -179,7 +209,7 @@
             [jnp.concatenate(cross_real, axis=0), jnp.concatenate(cross_imag, axis=0)],
             axis=1,
         ).astype(jnp.bfloat16)
-        inner[r] = jnp.dot(cross, table_ref[...], preferred_element_type=jnp.float32)
+        inner[r] = jnp.dot(cross, table[...], preferred_element_type=jnp.float32)
 
     window = lax.axis_index("win")
     mate = window + 1 - 2 * (window % 2)
@@ -276,19 +306,20 @@
     offsets = blocks // 4
     pairs = channels * channels
     group = 2 * pairs
-    twiddle = jnp.asarray(twiddles())
+    forward_twiddle = jnp.asarray(twiddles(SPLIT, SPAN))
+    twiddle = jnp.asarray(twiddles(RADIX, PERIOD))
     tables = jnp.asarray(np.stack(forward_tables()))
     series = traces.reshape(-1, LANES)
 
     own = call(
         functools.partial(whiten_kernel, rows),
         jax.ShapeDtypeStruct((rows, 2 * F), jnp.bfloat16),
-        *(pltpu.with_memory_space_constraint(x, pltpu.HBM) for x in (series, tables, twiddle)),
+        *(pltpu.with_memory_space_constraint(x, pltpu.HBM) for x in (series, tables, forward_twiddle)),
         specs=[HBM] * 3,
         scratch=(
             pltpu.VMEM(series.shape, jnp.float32),
             pltpu.VMEM(tables.shape, jnp.bfloat16),
-            pltpu.VMEM(twiddle.shape, jnp.float32),
+            pltpu.VMEM(forward_twiddle.shape, jnp.float32),
             pltpu.SemaphoreType.DMA((5,)),
         ),
     )
@@ -325,6 +356,7 @@
                 scratch=(
                     pltpu.VMEM((2 * rows, 2 * F), jnp.float32),
                     pltpu.VMEM((2 * rows, 2 * F), jnp.float32),
+                    pltpu.VMEM((2 * QS, 2 * PERIOD), jnp.bfloat16),
                     pltpu.VMEM((RADIX, segments * group, 2 * PERIOD), jnp.float32),
                 ),
             )

time: 17.1 us -> 16.7 us (0.977)
  Pallas kernels: 3.89 us -> 3.49 us
    pallas_call x4, Pallas kernels: 3.89 us -> 3.49 us  [call(): pl.pallas_call(kernel, out_shape=out, in_specs=[VMEM] * len(args) if spec...]
where the time goes in v3:
time: 16.7 us; the launch traced here: 16.6 us
  starting transfers between devices  7.18 us (43%)
  waiting for transfers between devices  5.84 us (35%)
  Pallas kernels  3.49 us (21%)
    ppermute x2, starting transfers between devices, from_block(): return lax.ppermute(array, ('chan', 'win'), moves)  5.16 us
    pallas_call x4, Pallas kernels, call(): pl.pallas_call(kernel, out_shape=out, in_specs=[VMEM] * len(args) if spec...  3.49 us
    ppermute x1, waiting for transfers between devices, shards(): lax.ppermute(stack, 'win', [(w, w ^ step) for w in range(windows)])  2.6 us
    ppermute x2, waiting for transfers between devices, from_block(): return lax.ppermute(array, ('chan', 'win'), moves)  2.4 us
    ppermute x1, starting transfers between devices, shards(): lax.ppermute(stack, 'win', [(w, w ^ step) for w in range(windows)])  1.56 us
    ppermute x2, waiting for transfers between devices, to_mate(): return lax.ppermute(array, 'win', [(w, w ^ 1) for w in range(windows)])  0.84 us
    ppermute x2, starting transfers between devices, to_mate(): return lax.ppermute(array, 'win', [(w, w ^ 1) for w in range(windows)])  0.46 us
  transfers between devices with their start and end apart: 5, of which 4 were waited for; matrix products, arithmetic and copies ran while one was open for 0% of the time, Pallas kernels for 0%

profile of v3, /device:TPU:0, one launch (start us, length us, event | category | flops | bytes accessed | tf_op | source)
XLA Modules:
  0.0 16.6 jit_solution(2717253496304777586)
XLA Ops:
  0.0 0.0 copy-start
  0.0 0.0 copy-start.1
  0.0 2.0 %shard_map.64.own_ref = bf16[24,1024]{1,0:T(8,128)(2,1)S(1)} custom-call(f32[384,128]{1,0:T(8,128)} %bitcast.7, bf16[3,512,128]{2,1,0:T(8,128)(2,1)} %constant.10.clone.tables_hbm, f32[16,256]{1,0:T(8,128)} %constant.8.clone.twiddle_hbm), custom_call_target="tpu_custom_call" | custom-call | tf_op jit(solution)/shard_map/pallas_call | solution.py:291
  2.0 0.0 copy-start.2
  2.0 3.5 %collective-permute-start.2 = (bf16[24,1024]{1,0:T(8,128)(2,1)S(1)}, bf16[24,1024]{1,0:T(8,128)(2,1)S(1)}, u32[]{:S(2)}, u32[]{:S(2)}) collective-permute-start(bf16[24,1024]{1,0:T(8,128)(2,1)S(1)} %shard_map.64.own_ref), channel_id=1, source_target_pairs={{5,0},{8,1},{7,2},{10,3},{9,4},{12,5},{11,6},{14,7},{13,8},{0,9},{... | collective-permute-start | bytes 147464 | tf_op jit(solution)/shard_map/ppermute | solution.py:336
  5.5 1.6 %collective-permute-start.1 = (bf16[24,1024]{1,0:T(8,128)(2,1)S(1)}, bf16[24,1024]{1,0:T(8,128)(2,1)S(1)}, u32[]{:S(2)}, u32[]{:S(2)}) collective-permute-start(bf16[24,1024]{1,0:T(8,128)(2,1)S(1)} %shard_map.64.own_ref), channel_id=1, source_target_pairs={{4,0},{9,1},{6,2},{11,3},{8,4},{13,5},{10,6},{15,7},{12,8},{1,9},{... | collective-permute-start | bytes 147464 | tf_op jit(solution)/shard_map/ppermute | solution.py:336
  7.2 0.1 collective-permute-start
  7.2 0.1 collective-permute-done.2.visitor_mate_ref
  7.3 2.3 %collective-permute-done.1.visitor_ref = bf16[24,1024]{1,0:T(8,128)(2,1)S(1)} collective-permute-done((bf16[24,1024]{1,0:T(8,128)(2,1)S(1)}, bf16[24,1024]{1,0:T(8,128)(2,1)S(1)}, u32[]{:S(2)}, u32[]{:S(2)}) %collective-permute-start.1) | collective-permute-done | bytes 49184 | tf_op jit(solution)/shard_map/ppermute | solution.py:336
  9.6 0.0 collective-permute-done.own_mate_ref
  9.6 0.0 copy-done
  9.6 0.0 copy-done.1
  9.6 0.0 copy-done.2
  9.7 0.8 %shard_map.65 = f32[24,512]{1,0:T(8,128)S(1)} custom-call(bf16[24,1024]{1,0:T(8,128)(2,1)S(1)} %shard_map.64.own_ref, bf16[24,1024]{1,0:T(8,128)(2,1)S(1)} %collective-permute-done.own_mate_ref, bf16[24,1024]{1,0:T(8,128)(2,1)S(1)} %collective-permute-done.1.visitor_ref, bf16[24,1024]{1,0:T(8,128)(2,1)S(1)} %collective-permute-done.2.visitor_mate_ref, ...), custom_call_target="tpu_custom_call" | custom-call | tf_op jit(solution)/shard_map/pallas_call | solution.py:291
  10.4 1.6 %collective-permute-start.3 = (f32[1,24,512]{2,1,0:T(8,128)S(1)}, f32[1,24,512]{2,1,0:T(8,128)S(1)}, u32[]{:S(2)}, u32[]{:S(2)}) collective-permute-start(f32[1,24,512]{2,1,0:T(8,128)S(1)} %bitcast.3), channel_id=1, source_target_pairs={{0,2},{1,3},{2,0},{3,1},{4,6},{5,7},{6,4},{7,5},{8,10},{9,11},{10,... | collective-permute-start | bytes 147464 | tf_op jit(solution)/shard_map/ppermute | solution.py:368
  12.0 2.6 %collective-permute-done.3.right_ref = f32[1,24,512]{2,1,0:T(8,128)S(1)} collective-permute-done((f32[1,24,512]{2,1,0:T(8,128)S(1)}, f32[1,24,512]{2,1,0:T(8,128)S(1)}, u32[]{:S(2)}, u32[]{:S(2)}) %collective-permute-start.3) | collective-permute-done | bytes 49184 | tf_op jit(solution)/shard_map/ppermute | solution.py:368
  14.6 0.1 shard_map.66.own_ref
  14.7 0.4 %collective-permute-start.4 = (f32[1,8,512]{2,1,0:T(8,128)S(1)}, f32[1,8,512]{2,1,0:T(8,128)S(1)}, u32[]{:S(2)}, u32[]{:S(2)}) collective-permute-start(f32[1,8,512]{2,1,0:T(8,128)S(1)} %shard_map.66.own_ref), channel_id=1, source_target_pairs={{0,1},{1,0},{2,3},{3,2},{4,5},{5,4},{6,7},{7,6},{8,9},{9,8},{10,11... | collective-permute-start | bytes 49160 | tf_op jit(solution)/shard_map/ppermute | solution.py:328
  15.1 0.8 %collective-permute-done.4.mate_ref = f32[1,8,512]{2,1,0:T(8,128)S(1)} collective-permute-done((f32[1,8,512]{2,1,0:T(8,128)S(1)}, f32[1,8,512]{2,1,0:T(8,128)S(1)}, u32[]{:S(2)}, u32[]{:S(2)}) %collective-permute-start.4) | collective-permute-done | bytes 16416 | tf_op jit(solution)/shard_map/ppermute | solution.py:328
  15.9 0.6 %shard_map.67 = f32[1,2,2,2,1024]{4,3,2,1,0:T(2,128)} custom-call(f32[1,8,512]{2,1,0:T(8,128)S(1)} %shard_map.66.own_ref, f32[1,8,512]{2,1,0:T(8,128)S(1)} %collective-permute-done.4.mate_ref), custom_call_target="tpu_custom_call" | custom-call | tf_op jit(solution)/shard_map/pallas_call | solution.py:291
Async XLA Ops:
  0.0 9.6 %copy-start = (bf16[128,1024]{1,0:T(8,128)(2,1)S(1)}, bf16[128,1024]{1,0:T(8,128)(2,1)}, u32[]{:S(2)}) copy-start(bf16[128,1024]{1,0:T(8,128)(2,1)} %constant.11.clone.table_ref) | copy-start | bytes 786436
  0.0 9.6 %copy-start.1 = (f32[8,512]{1,0:T(8,128)S(1)}, f32[8,512]{1,0:T(8,128)}, u32[]{:S(2)}) copy-start(f32[8,512]{1,0:T(8,128)} %constant.9.clone.twiddle_ref) | copy-start | bytes 49156
  2.0 7.6 %copy-start.2 = (s32[4]{0:T(128)S(1)}, s32[4]{0:T(128)}, u32[]{:S(2)}) copy-start(s32[4]{0:T(128)} %param.7) | copy-start | bytes 52
  2.0 5.3 %collective-permute-start.2 = (bf16[24,1024]{1,0:T(8,128)(2,1)S(1)}, bf16[24,1024]{1,0:T(8,128)(2,1)S(1)}, u32[]{:S(2)}, u32[]{:S(2)}) collective-permute-start(bf16[24,1024]{1,0:T(8,128)(2,1)S(1)} %shard_map.64.own_ref), channel_id=1, source_target_pairs={{5,0},{8,1},{7,2},{10,3},{9,4},{12,5},{11,6},{14,7},{13,8},{0,9},{... | collective-permute-start | bytes 147464 | tf_op jit(solution)/shard_map/ppermute | solution.py:336
  5.5 4.1 %collective-permute-start.1 = (bf16[24,1024]{1,0:T(8,128)(2,1)S(1)}, bf16[24,1024]{1,0:T(8,128)(2,1)S(1)}, u32[]{:S(2)}, u32[]{:S(2)}) collective-permute-start(bf16[24,1024]{1,0:T(8,128)(2,1)S(1)} %shard_map.64.own_ref), channel_id=1, source_target_pairs={{4,0},{9,1},{6,2},{11,3},{8,4},{13,5},{10,6},{15,7},{12,8},{1,9},{... | collective-permute-start | bytes 147464 | tf_op jit(solution)/shard_map/ppermute | solution.py:336
  7.2 2.5 %collective-permute-start = (bf16[24,1024]{1,0:T(8,128)(2,1)S(1)}, bf16[24,1024]{1,0:T(8,128)(2,1)S(1)}, u32[]{:S(2)}, u32[]{:S(2)}) collective-permute-start(bf16[24,1024]{1,0:T(8,128)(2,1)S(1)} %shard_map.64.own_ref), channel_id=1, source_target_pairs={{0,1},{1,0},{2,3},{3,2},{4,5},{5,4},{6,7},{7,6},{8,9},{9,8},{10,11... | collective-permute-start | bytes 147464 | tf_op jit(solution)/shard_map/ppermute | solution.py:328
  10.4 4.2 %collective-permute-start.3 = (f32[1,24,512]{2,1,0:T(8,128)S(1)}, f32[1,24,512]{2,1,0:T(8,128)S(1)}, u32[]{:S(2)}, u32[]{:S(2)}) collective-permute-start(f32[1,24,512]{2,1,0:T(8,128)S(1)} %bitcast.3), channel_id=1, source_target_pairs={{0,2},{1,3},{2,0},{3,1},{4,6},{5,7},{6,4},{7,5},{8,10},{9,11},{10,... | collective-permute-start | bytes 147464 | tf_op jit(solution)/shard_map/ppermute | solution.py:368
  14.7 1.2 %collective-permute-start.4 = (f32[1,8,512]{2,1,0:T(8,128)S(1)}, f32[1,8,512]{2,1,0:T(8,128)S(1)}, u32[]{:S(2)}, u32[]{:S(2)}) collective-permute-start(f32[1,8,512]{2,1,0:T(8,128)S(1)} %shard_map.66.own_ref), channel_id=1, source_target_pairs={{0,1},{1,0},{2,3},{3,2},{4,5},{5,4},{6,7},{7,6},{8,9},{9,8},{10,11... | collective-permute-start | bytes 49160 | tf_op jit(solution)/shard_map/ppermute | solution.py:328

commit v4 on v3

--- a/solution.py
+++ b/solution.py
@@ -38,17 +38,20 @@
     return parts
 
 
-def forward_tables():
+def forward_table():
     t0 = np.arange(SPAN)
     angle = (t0[:, None] * FORWARD_Q[None, :] % SPAN) * (2 * math.pi / SPAN)
-    cosine, sine = np.cos(angle), np.sin(angle)
-    return split_three(np.block([[cosine, -sine], [sine, cosine]]))
+    parts = split_three(np.block([np.cos(angle), np.sin(angle)]))
+    return np.concatenate(parts, axis=1)
 
 
 def backward_table():
     m = np.arange(PERIOD)
     angle = (BACKWARD_Q[:, None] * m[None, :] % PERIOD) * (2 * math.pi / PERIOD)
-    table = np.block([np.cos(angle), np.sin(angle)]) / math.sqrt(F)
+    cosine, sine = np.cos(angle), np.sin(angle)
+    halves = np.array([np.block([[cosine], [-sine]]), np.block([[sine], [cosine]])])
+    table = halves.reshape(2, 2 * QS, -1, LANES).transpose(1, 2, 0, 3)
+    table = table.reshape(2 * QS, 2 * PERIOD) / math.sqrt(F)
     return table.astype(np.float32).astype(jnp.bfloat16)
 
 
@@ -84,20 +87,55 @@
 
 
 def whiten_kernel(
-    rows, x_hbm, tables_hbm, twiddle_hbm, out_ref, x_ref, tables, twiddle_ref, sems
+    rows,
+    pairs,
+    x_hbm,
+    table_hbm,
+    twiddle_hbm,
+    count_hbm,
+    backward_hbm,
+    backward_twiddle_hbm,
+    out_ref,
+    kept_ref,
+    square_ref,
+    backward_ref,
+    backward_twiddle_ref,
+    x_ref,
+    table,
+    twiddle_ref,
+    count_ref,
+    sems,
 ):
     copies = [
         pltpu.make_async_copy(x_hbm, x_ref, sems.at[0]),
         pltpu.make_async_copy(twiddle_hbm, twiddle_ref, sems.at[1]),
+        pltpu.make_async_copy(table_hbm, table, sems.at[2]),
+        pltpu.make_async_copy(count_hbm, count_ref, sems.at[3]),
     ]
-    copies += [
-        pltpu.make_async_copy(tables_hbm.at[i], tables.at[i], sems.at[2 + i])
-        for i in range(3)
+    later = [
+        pltpu.make_async_copy(backward_hbm, backward_ref, sems.at[4]),
+        pltpu.make_async_copy(backward_twiddle_hbm, backward_twiddle_ref, sems.at[5]),
     ]
-    for copy in copies:
+    for copy in copies + later:
         copy.start()
     for copy in copies:
         copy.wait()
+
+    window = lax.axis_index("win")
+    mate = window + 1 - 2 * (window % 2)
+    counts = count_ref[...]
+    lane = lax.broadcasted_iota(jnp.int32, counts.shape, 1)
+    own_count, mate_count = (
+        jnp.sum(jnp.where(lane == w, counts, 0), axis=1, keepdims=True)
+        for w in (window, mate)
+    )
+    group = 2 * pairs
+    is_own = lax.broadcasted_iota(jnp.int32, (group, LANES), 0) < pairs
+    count = jnp.where(is_own, own_count, mate_count)
+    for k in range(kept_ref.shape[0] // group):
+        kept_ref[k * group : (k + 1) * group] = (count > k).astype(jnp.float32)
+    total = jnp.sum(counts, axis=1, keepdims=True).astype(jnp.float32)
+    square_ref[...] = jnp.broadcast_to(total * total, square_ref.shape)
 
     chunks = SPAN // LANES
     real = [[] for _ in range(SPLIT)]
@@ -110,30 +148,38 @@
         for r, (re, im) in enumerate(eight_points(x)):
             if r > 0:
                 cosine, sine = (
-                    twiddle_ref[2 * r - 2 + i, c * LANES : (c + 1) * LANES].reshape(1, LANES)
+                    twiddle_ref[2 * r - 2 + i : 2 * r - 1 + i, c * LANES : (c + 1) * LANES]
                     for i in range(2)
                 )
                 if im is None:
                     re, im = re * cosine, -(re * sine)
                 else:
                     re, im = re * cosine + im * sine, im * cosine - re * sine
+                imag[r].append(im)
             real[r].append(re)
-            imag[r].append(jnp.zeros_like(re) if im is None else im)
     series = jnp.concatenate(
-        [jnp.concatenate(real[r] + imag[r], axis=1) for r in range(SPLIT)], axis=0
+        [jnp.concatenate(part, axis=1) for part in real + imag[1:]], axis=0
     )
     high = series.astype(jnp.bfloat16)
     rest = series - high.astype(jnp.float32)
     mid = rest.astype(jnp.bfloat16)
     low = (rest - mid.astype(jnp.float32)).astype(jnp.bfloat16)
     dot = functools.partial(jnp.dot, preferred_element_type=jnp.float32)
-    n = SPLIT * rows
-    by_high = dot(jnp.concatenate([high, mid, low], axis=0), tables[0])
-    by_mid = dot(jnp.concatenate([high, mid], axis=0), tables[1])
-    by_low = dot(high, tables[2])
-    small = by_high[2 * n :] + by_mid[n:] + by_low
-    spectra = by_high[:n] + ((by_high[n : 2 * n] + by_mid[:n]) + small)
-    blocks = [spectra[r * rows : (r + 1) * rows] for r in range(SPLIT)]
+    width = 2 * NARROW
+    n = series.shape[0]
+    both = dot(jnp.concatenate([high, mid, low], axis=0), table[:, : 2 * width])
+    small = dot(high, table[:, 2 * width :])
+    small = small + (both[n : 2 * n, width:] + both[2 * n :, :width])
+    product = both[:n, :width] + ((both[:n, width:] + both[n : 2 * n, :width]) + small)
+    left = lax.broadcasted_iota(jnp.int32, (rows, LANES), 1) < NARROW
+    blocks = []
+    for r in range(SPLIT):
+        block = product[r * rows : (r + 1) * rows]
+        block = jnp.where(left, block, -block)
+        if r > 0:
+            at = (SPLIT + r - 1) * rows
+            block = block + pltpu.roll(product[at : at + rows], NARROW, axis=1)
+        blocks.append(block)
     power = []
     for block in blocks:
         square = block * block
@@ -143,7 +189,6 @@
     )
     mean = jnp.sum(total, axis=1, keepdims=True) * (0.5 / F)
     floor = 0.09 * (mean + 1e-06)
-    left = lax.broadcasted_iota(jnp.int32, (rows, LANES), 1) < NARROW
     white = [b * lax.rsqrt(jnp.maximum(p, floor)) for b, p in zip(blocks, power)]
     for r in range(RADIX):
         first, second = white[r], white[r + RADIX]
@@ -152,6 +197,8 @@
         im = jnp.where(left, pltpu.roll(first, NARROW, axis=1), second)
         out_ref[:, at : at + QS] = re.astype(jnp.bfloat16)
         out_ref[:, at + QS : at + 2 * QS] = im.astype(jnp.bfloat16)
+    for copy in later:
+        copy.wait()
 
 
 def stack_kernel(
@@ -161,13 +208,13 @@
     own_mate_ref,
     visitor_ref,
     visitor_mate_ref,
-    count_ref,
+    kept_ref,
     table_ref,
     twiddle_ref,
     out_ref,
     own,
     visitor,
-    table,
+    cross,
     inner,
 ):
     rows = channels * segments
@@ -177,10 +224,6 @@
     own[rows : 2 * rows] = own_mate_ref[...].astype(jnp.float32)
     visitor[0:rows] = visitor_ref[...].astype(jnp.float32)
     visitor[rows : 2 * rows] = visitor_mate_ref[...].astype(jnp.float32)
-
-    table[0:QS] = table_ref[...]
-    table[QS : 2 * QS, 0:PERIOD] = -table_ref[:, PERIOD:]
-    table[QS : 2 * QS, PERIOD:] = table_ref[:, 0:PERIOD]
 
     place = lax.broadcasted_iota(jnp.int32, (group, LANES), 0)
     own_of = place // channels
@@ -205,22 +248,18 @@
             vis_im = spread(visitor, visitor_of, k, at + QS)
             cross_real.append(own_re * vis_re + own_im * vis_im)
             cross_imag.append(own_im * vis_re - own_re * vis_im)
-        cross = jnp.concatenate(
-            [jnp.concatenate(cross_real, axis=0), jnp.concatenate(cross_imag, axis=0)],
-            axis=1,
-        ).astype(jnp.bfloat16)
-        inner[r] = jnp.dot(cross, table[...], preferred_element_type=jnp.float32)
-
-    window = lax.axis_index("win")
-    mate = window + 1 - 2 * (window % 2)
-    counts = count_ref[...]
-    lane = lax.broadcasted_iota(jnp.int32, counts.shape, 1)
-    kept_own, kept_mate = (
-        jnp.sum(jnp.where(lane == w, counts, 0), axis=1, keepdims=True)
-        for w in (window, mate)
-    )
-    kept_count = jnp.where(is_own, kept_own, kept_mate)
-    kept = [(kept_count > k).astype(jnp.float32) for k in range(segments)]
+        at = slice(r * segments * group, (r + 1) * segments * group)
+        cross[at, 0:QS] = jnp.concatenate(cross_real, axis=0).astype(jnp.bfloat16)
+        cross[at, QS:] = jnp.concatenate(cross_imag, axis=0).astype(jnp.bfloat16)
+
+    for c in range(PERIOD // LANES):
+        inner[c] = jnp.dot(
+            cross[...],
+            table_ref[:, 2 * c * LANES : 2 * (c + 1) * LANES],
+            preferred_element_type=jnp.float32,
+        )
+
+    kept = [kept_ref[k * group : (k + 1) * group] for k in range(segments)]
 
     for c in range(PERIOD // LANES):
         low, high = c * LANES, (c + 1) * LANES
@@ -230,9 +269,13 @@
         )
         sums = [[None] * 3, [None] * 3]
         for k in range(segments):
-            at = slice(k * group, (k + 1) * group)
-            re = [inner[r, at, low:high] for r in range(RADIX)]
-            im = [inner[r, at, PERIOD + low : PERIOD + high] for r in range(RADIX)]
+            re, im = (
+                [
+                    inner[c, pl.ds((r * segments + k) * group, group), half]
+                    for r in range(RADIX)
+                ]
+                for half in (slice(0, LANES), slice(LANES, 2 * LANES))
+            )
             re1, im1 = re[1] * cos1 - im[1] * sin1, re[1] * sin1 + im[1] * cos1
             re2, im2 = re[2] * cos2 - im[2] * sin2, re[2] * sin2 + im[2] * cos2
             re3, im3 = re[3] * cos3 - im[3] * sin3, re[3] * sin3 + im[3] * cos3
@@ -259,17 +302,18 @@
     out_ref[...] = left_ref[...] + right_ref[...]
 
 
-def result_kernel(left_ref, right_ref, count_ref, out_ref):
-    total = jnp.sum(count_ref[...], axis=1, keepdims=True).astype(jnp.float32)
-    square = total * total
+def result_kernel(left_ref, right_ref, square_ref, out_ref):
     group = out_ref.shape[1]
     for offset in range(out_ref.shape[0]):
-        linear, cos_sum, sin_sum = (
-            left_ref[offset, i * group : (i + 1) * group]
-            + right_ref[offset, i * group : (i + 1) * group]
-            for i in range(3)
-        )
-        out_ref[offset] = linear * (cos_sum * cos_sum + sin_sum * sin_sum) / square
+        for low in range(0, out_ref.shape[2], LANES):
+            at = slice(low, low + LANES)
+            linear, cos_sum, sin_sum = (
+                left_ref[offset, i * group : (i + 1) * group, at]
+                + right_ref[offset, i * group : (i + 1) * group, at]
+                for i in range(3)
+            )
+            power = cos_sum * cos_sum + sin_sum * sin_sum
+            out_ref[offset, :, at] = linear * power / square_ref[...]
 
 
 def join_kernel(own_ref, mate_ref, out_ref):
@@ -292,7 +336,7 @@
         kernel,
         out_shape=out,
         in_specs=[VMEM] * len(args) if specs is None else specs,
-        out_specs=VMEM,
+        out_specs=jax.tree.map(lambda _: VMEM, out),
         scratch_shapes=list(scratch),
         compiler_params=pltpu.CompilerParams(vmem_limit_bytes=limit),
     )(*args)
@@ -308,19 +352,26 @@
     group = 2 * pairs
     forward_twiddle = jnp.asarray(twiddles(SPLIT, SPAN))
     twiddle = jnp.asarray(twiddles(RADIX, PERIOD))
-    tables = jnp.asarray(np.stack(forward_tables()))
+    forward = jnp.asarray(forward_table())
     series = traces.reshape(-1, LANES)
 
-    own = call(
-        functools.partial(whiten_kernel, rows),
-        jax.ShapeDtypeStruct((rows, 2 * F), jnp.bfloat16),
-        *(pltpu.with_memory_space_constraint(x, pltpu.HBM) for x in (series, tables, forward_twiddle)),
-        specs=[HBM] * 3,
+    counts = seg_count.reshape(1, -1)
+    backward = jnp.asarray(backward_table())
+    inputs = (series, forward, forward_twiddle, counts)
+    inputs_on = (backward, twiddle)
+    own, kept, square, backward, twiddle = call(
+        functools.partial(whiten_kernel, rows, pairs),
+        (
+            jax.ShapeDtypeStruct((rows, 2 * F), jnp.bfloat16),
+            jax.ShapeDtypeStruct((segments * group, LANES), jnp.float32),
+            jax.ShapeDtypeStruct((group, LANES), jnp.float32),
+            *(jax.ShapeDtypeStruct(x.shape, x.dtype) for x in inputs_on),
+        ),
+        *(pltpu.with_memory_space_constraint(x, pltpu.HBM) for x in inputs + inputs_on),
+        specs=[HBM] * 6,
         scratch=(
-            pltpu.VMEM(series.shape, jnp.float32),
-            pltpu.VMEM(tables.shape, jnp.bfloat16),
-            pltpu.VMEM(forward_twiddle.shape, jnp.float32),
-            pltpu.SemaphoreType.DMA((5,)),
+            *(pltpu.VMEM(x.shape, x.dtype) for x in inputs),
+            pltpu.SemaphoreType.DMA((6,)),
         ),
     )
 
@@ -335,8 +386,6 @@
                 moves.append((source, z * windows + w))
         return lax.ppermute(array, ("chan", "win"), moves)
 
-    counts = seg_count.reshape(1, -1)
-    backward = jnp.asarray(backward_table())
     own_mate = to_mate(own)
     stacks = []
     for j in range(offsets):
@@ -350,14 +399,17 @@
                 own_mate,
                 visitor,
                 visitor_mate,
-                counts,
+                kept,
                 backward,
                 twiddle,
                 scratch=(
                     pltpu.VMEM((2 * rows, 2 * F), jnp.float32),
                     pltpu.VMEM((2 * rows, 2 * F), jnp.float32),
-                    pltpu.VMEM((2 * QS, 2 * PERIOD), jnp.bfloat16),
-                    pltpu.VMEM((RADIX, segments * group, 2 * PERIOD), jnp.float32),
+                    pltpu.VMEM((RADIX * segments * group, 2 * QS), jnp.bfloat16),
+                    pltpu.VMEM(
+                        (PERIOD // LANES, RADIX * segments * group, 2 * LANES),
+                        jnp.float32,
+                    ),
                 ),
             )
         )
@@ -377,7 +429,7 @@
         jax.ShapeDtypeStruct((offsets, group, PERIOD), jnp.float32),
         stack,
         arrived,
-        counts,
+        square,
     )
     return call(
         join_kernel,

time: 16.7 us -> 16.4 us (0.982)
  Pallas kernels: 3.49 us -> 3.16 us
    pallas_call x4, Pallas kernels: 3.49 us -> 3.16 us  [call(): pl.pallas_call(kernel, out_shape=out, in_specs=[VMEM] * len(args) if spec...]
where the time goes in v4:
time: 16.4 us; the launch traced here: 16.3 us
  starting transfers between devices  7.24 us (44%)
  waiting for transfers between devices  5.84 us (36%)
  Pallas kernels  3.16 us (19%)
    ppermute x2, starting transfers between devices, from_block(): return lax.ppermute(array, ('chan', 'win'), moves)  5.16 us
    pallas_call x4, Pallas kernels, call(): pl.pallas_call(kernel, out_shape=out, in_specs=[VMEM] * len(args) if spec...  3.16 us
    ppermute x1, waiting for transfers between devices, shards(): lax.ppermute(stack, 'win', [(w, w ^ step) for w in range(windows)])  2.6 us
    ppermute x2, waiting for transfers between devices, from_block(): return lax.ppermute(array, ('chan', 'win'), moves)  2.4 us
    ppermute x1, starting transfers between devices, shards(): lax.ppermute(stack, 'win', [(w, w ^ step) for w in range(windows)])  1.55 us
    ppermute x2, waiting for transfers between devices, to_mate(): return lax.ppermute(array, 'win', [(w, w ^ 1) for w in range(windows)])  0.84 us
    ppermute x2, starting transfers between devices, to_mate(): return lax.ppermute(array, 'win', [(w, w ^ 1) for w in range(windows)])  0.52 us
  transfers between devices with their start and end apart: 5, of which 4 were waited for; matrix products, arithmetic and copies ran while one was open for 0% of the time, Pallas kernels for 0%

profile of v4, /device:TPU:0, one launch (start us, length us, event | category | flops | bytes accessed | tf_op | source)
XLA Modules:
  0.0 16.3 jit_solution(17093942412798072454)
XLA Ops:
  0.0 1.8 %shard_map.64 = (bf16[24,1024]{1,0:T(8,128)(2,1)S(1)}, f32[96,128]{1,0:T(8,128)S(1)}, f32[8,128]{1,0:T(8,128)S(1)}, bf16[256,1024]{1,0:T(8,128)(2,1)S(1)}, f32[8,512]{1,0:T(8,128)S(1)}) custom-call(f32[384,128]{1,0:T(8,128)} %bitcast.5, bf16[256,384]{1,0:T(8,128)(2,1)} %constant.10.clone.table_hbm, f32[16,256]{1,0:T(8,128)} %constant.8.clone.twiddle_hbm, ...), custom_call_target="tpu_custom_call" | custom-call | tf_op jit(solution)/shard_map/pallas_call | solution.py:335
  1.8 3.5 %collective-permute-start.2 = (bf16[24,1024]{1,0:T(8,128)(2,1)S(1)}, bf16[24,1024]{1,0:T(8,128)(2,1)S(1)}, u32[]{:S(2)}, u32[]{:S(2)}) collective-permute-start(bf16[24,1024]{1,0:T(8,128)(2,1)S(1)} %get-tuple-element.10.own_ref), channel_id=1, source_target_pairs={{5,0},{8,1},{7,2},{10,3},{9,4},{12,5},{11,6},{14,7},{13,8},{0,9},{... | collective-permute-start | bytes 147464 | tf_op jit(solution)/shard_map/ppermute | solution.py:387
  5.3 1.6 %collective-permute-start.1 = (bf16[24,1024]{1,0:T(8,128)(2,1)S(1)}, bf16[24,1024]{1,0:T(8,128)(2,1)S(1)}, u32[]{:S(2)}, u32[]{:S(2)}) collective-permute-start(bf16[24,1024]{1,0:T(8,128)(2,1)S(1)} %get-tuple-element.10.own_ref), channel_id=1, source_target_pairs={{4,0},{9,1},{6,2},{11,3},{8,4},{13,5},{10,6},{15,7},{12,8},{1,9},{... | collective-permute-start | bytes 147464 | tf_op jit(solution)/shard_map/ppermute | solution.py:387
  7.0 0.1 collective-permute-start
  7.0 0.1 collective-permute-done.2.visitor_mate_ref
  7.1 2.3 %collective-permute-done.1.visitor_ref = bf16[24,1024]{1,0:T(8,128)(2,1)S(1)} collective-permute-done((bf16[24,1024]{1,0:T(8,128)(2,1)S(1)}, bf16[24,1024]{1,0:T(8,128)(2,1)S(1)}, u32[]{:S(2)}, u32[]{:S(2)}) %collective-permute-start.1) | collective-permute-done | bytes 49184 | tf_op jit(solution)/shard_map/ppermute | solution.py:387
  9.4 0.0 collective-permute-done.own_mate_ref
  9.4 0.7 %shard_map.65 = f32[24,512]{1,0:T(8,128)S(1)} custom-call(bf16[24,1024]{1,0:T(8,128)(2,1)S(1)} %get-tuple-element.10.own_ref, bf16[24,1024]{1,0:T(8,128)(2,1)S(1)} %collective-permute-done.own_mate_ref, bf16[24,1024]{1,0:T(8,128)(2,1)S(1)} %collective-permute-done.1.visitor_ref, bf16[24,1024]{1,0:T(8,128)(2,1)S(1)} %collective-permute-done.2.visitor_mate_ref, ...), custom_call_target="tpu_custom_call" | custom-call | tf_op jit(solution)/shard_map/pallas_call | solution.py:335
  10.2 1.6 %collective-permute-start.3 = (f32[1,24,512]{2,1,0:T(8,128)S(1)}, f32[1,24,512]{2,1,0:T(8,128)S(1)}, u32[]{:S(2)}, u32[]{:S(2)}) collective-permute-start(f32[1,24,512]{2,1,0:T(8,128)S(1)} %bitcast.3), channel_id=1, source_target_pairs={{0,2},{1,3},{2,0},{3,1},{4,6},{5,7},{6,4},{7,5},{8,10},{9,11},{10,... | collective-permute-start | bytes 147464 | tf_op jit(solution)/shard_map/ppermute | solution.py:420
  11.7 2.6 %collective-permute-done.3.right_ref = f32[1,24,512]{2,1,0:T(8,128)S(1)} collective-permute-done((f32[1,24,512]{2,1,0:T(8,128)S(1)}, f32[1,24,512]{2,1,0:T(8,128)S(1)}, u32[]{:S(2)}, u32[]{:S(2)}) %collective-permute-start.3) | collective-permute-done | bytes 49184 | tf_op jit(solution)/shard_map/ppermute | solution.py:420
  14.3 0.5 %collective-permute-start.4 = (f32[1,8,512]{2,1,0:T(8,128)S(1)}, f32[1,8,512]{2,1,0:T(8,128)S(1)}, u32[]{:S(2)}, u32[]{:S(2)}) collective-permute-start(f32[1,8,512]{2,1,0:T(8,128)S(1)} %shard_map.66.own_ref), channel_id=1, source_target_pairs={{0,1},{1,0},{2,3},{3,2},{4,5},{5,4},{6,7},{7,6},{8,9},{9,8},{10,11... | collective-permute-start | bytes 49160 | tf_op jit(solution)/shard_map/ppermute | solution.py:379
  14.8 0.8 %collective-permute-done.4.mate_ref = f32[1,8,512]{2,1,0:T(8,128)S(1)} collective-permute-done((f32[1,8,512]{2,1,0:T(8,128)S(1)}, f32[1,8,512]{2,1,0:T(8,128)S(1)}, u32[]{:S(2)}, u32[]{:S(2)}) %collective-permute-start.4) | collective-permute-done | bytes 16416 | tf_op jit(solution)/shard_map/ppermute | solution.py:379
  15.6 0.6 %shard_map.67 = f32[1,2,2,2,1024]{4,3,2,1,0:T(2,128)} custom-call(f32[1,8,512]{2,1,0:T(8,128)S(1)} %shard_map.66.own_ref, f32[1,8,512]{2,1,0:T(8,128)S(1)} %collective-permute-done.4.mate_ref), custom_call_target="tpu_custom_call" | custom-call | tf_op jit(solution)/shard_map/pallas_call | solution.py:335
  (1 shorter events, 0.0 us)
Async XLA Ops:
  1.8 5.3 %collective-permute-start.2 = (bf16[24,1024]{1,0:T(8,128)(2,1)S(1)}, bf16[24,1024]{1,0:T(8,128)(2,1)S(1)}, u32[]{:S(2)}, u32[]{:S(2)}) collective-permute-start(bf16[24,1024]{1,0:T(8,128)(2,1)S(1)} %get-tuple-element.10.own_ref), channel_id=1, source_target_pairs={{5,0},{8,1},{7,2},{10,3},{9,4},{12,5},{11,6},{14,7},{13,8},{0,9},{... | collective-permute-start | bytes 147464 | tf_op jit(solution)/shard_map/ppermute | solution.py:387
  5.3 4.1 %collective-permute-start.1 = (bf16[24,1024]{1,0:T(8,128)(2,1)S(1)}, bf16[24,1024]{1,0:T(8,128)(2,1)S(1)}, u32[]{:S(2)}, u32[]{:S(2)}) collective-permute-start(bf16[24,1024]{1,0:T(8,128)(2,1)S(1)} %get-tuple-element.10.own_ref), channel_id=1, source_target_pairs={{4,0},{9,1},{6,2},{11,3},{8,4},{13,5},{10,6},{15,7},{12,8},{1,9},{... | collective-permute-start | bytes 147464 | tf_op jit(solution)/shard_map/ppermute | solution.py:387
  7.0 2.5 %collective-permute-start = (bf16[24,1024]{1,0:T(8,128)(2,1)S(1)}, bf16[24,1024]{1,0:T(8,128)(2,1)S(1)}, u32[]{:S(2)}, u32[]{:S(2)}) collective-permute-start(bf16[24,1024]{1,0:T(8,128)(2,1)S(1)} %get-tuple-element.10.own_ref), channel_id=1, source_target_pairs={{0,1},{1,0},{2,3},{3,2},{4,5},{5,4},{6,7},{7,6},{8,9},{9,8},{10,11... | collective-permute-start | bytes 147464 | tf_op jit(solution)/shard_map/ppermute | solution.py:379
  10.2 4.2 %collective-permute-start.3 = (f32[1,24,512]{2,1,0:T(8,128)S(1)}, f32[1,24,512]{2,1,0:T(8,128)S(1)}, u32[]{:S(2)}, u32[]{:S(2)}) collective-permute-start(f32[1,24,512]{2,1,0:T(8,128)S(1)} %bitcast.3), channel_id=1, source_target_pairs={{0,2},{1,3},{2,0},{3,1},{4,6},{5,7},{6,4},{7,5},{8,10},{9,11},{10,... | collective-permute-start | bytes 147464 | tf_op jit(solution)/shard_map/ppermute | solution.py:420
  14.3 1.3 %collective-permute-start.4 = (f32[1,8,512]{2,1,0:T(8,128)S(1)}, f32[1,8,512]{2,1,0:T(8,128)S(1)}, u32[]{:S(2)}, u32[]{:S(2)}) collective-permute-start(f32[1,8,512]{2,1,0:T(8,128)S(1)} %shard_map.66.own_ref), channel_id=1, source_target_pairs={{0,1},{1,0},{2,3},{3,2},{4,5},{5,4},{6,7},{7,6},{8,9},{9,8},{10,11... | collective-permute-start | bytes 49160 | tf_op jit(solution)/shard_map/ppermute | solution.py:379

commit v5 on v4

--- a/solution.py
+++ b/solution.py
@@ -26,6 +26,10 @@
 
 VMEM = pl.BlockSpec(memory_space=pltpu.VMEM)
 HBM = pl.BlockSpec(memory_space=pltpu.HBM)
+
+
+def side(block, core, blocks):
+    return (core + block // (blocks // 2)) % 2
 
 
 def split_three(table):
@@ -206,8 +210,8 @@
     segments,
     own_ref,
     own_mate_ref,
-    visitor_ref,
-    visitor_mate_ref,
+    second_ref,
+    first_ref,
     kept_ref,
     table_ref,
     twiddle_ref,
@@ -222,8 +226,11 @@
     group = 2 * pairs
     own[0:rows] = own_ref[...].astype(jnp.float32)
     own[rows : 2 * rows] = own_mate_ref[...].astype(jnp.float32)
-    visitor[0:rows] = visitor_ref[...].astype(jnp.float32)
-    visitor[rows : 2 * rows] = visitor_mate_ref[...].astype(jnp.float32)
+    mine = (lax.axis_index("chan") + lax.axis_index("win")) % 2 == 0
+    at = jnp.where(mine, 0, rows)
+    for ref, start in ((first_ref, at), (second_ref, rows - at)):
+        start = pl.multiple_of(start, 8)
+        visitor[pl.ds(start, rows)] = ref[...].astype(jnp.float32)
 
     place = lax.broadcasted_iota(jnp.int32, (group, LANES), 0)
     own_of = place // channels
@@ -252,16 +259,19 @@
         cross[at, 0:QS] = jnp.concatenate(cross_real, axis=0).astype(jnp.bfloat16)
         cross[at, QS:] = jnp.concatenate(cross_imag, axis=0).astype(jnp.bfloat16)
 
-    for c in range(PERIOD // LANES):
+    def product(c):
         inner[c] = jnp.dot(
             cross[...],
             table_ref[:, 2 * c * LANES : 2 * (c + 1) * LANES],
             preferred_element_type=jnp.float32,
         )
 
+    product(0)
     kept = [kept_ref[k * group : (k + 1) * group] for k in range(segments)]
 
     for c in range(PERIOD // LANES):
+        if c + 1 < PERIOD // LANES:
+            product(c + 1)
         low, high = c * LANES, (c + 1) * LANES
         cos1, sin1, cos2, sin2, cos3, sin3 = (
             jnp.broadcast_to(twiddle_ref[i : i + 1, low:high], (group, LANES))
@@ -316,17 +326,17 @@
             out_ref[offset, :, at] = linear * power / square_ref[...]
 
 
-def join_kernel(own_ref, mate_ref, out_ref):
-    core = lax.axis_index("win") % 2
+def join_kernel(blocks, own_ref, mate_ref, out_ref):
+    parity = side(lax.axis_index("chan"), lax.axis_index("win") % 2, blocks)
     channels = out_ref.shape[2]
     half_lags = own_ref.shape[2]
-    for ref, parity in ((own_ref, core), (mate_ref, 1 - core)):
+    for ref, place in ((own_ref, 1 - parity), (mate_ref, parity)):
         for offset in range(own_ref.shape[0]):
             for half in range(2):
                 for a in range(channels):
                     row = (half * channels + a) * channels
                     lags = slice(half * half_lags, (half + 1) * half_lags)
-                    out_ref[0, 2 * offset + parity, a, :, lags] = ref[
+                    out_ref[0, 2 * offset + place, a, :, lags] = ref[
                         offset, row : row + channels
                     ]
 
@@ -382,23 +392,24 @@
         moves = []
         for z in range(blocks):
             for w in range(windows):
-                source = (z + offset + w % 2) % blocks * windows + (w ^ flip)
+                block = (z + offset + side(z, w % 2, blocks)) % blocks
+                source = block * windows + w // 2 * 2 + (z % 2 ^ flip)
                 moves.append((source, z * windows + w))
         return lax.ppermute(array, ("chan", "win"), moves)
 
     own_mate = to_mate(own)
     stacks = []
     for j in range(offsets):
-        visitor = from_block(own, 1 + 2 * j, 0)
-        visitor_mate = from_block(own, 1 + 2 * j, 1)
+        second = from_block(own, 1 + 2 * j, 1)
+        first = from_block(own, 1 + 2 * j, 0)
         stacks.append(
             call(
                 functools.partial(stack_kernel, channels, segments),
                 jax.ShapeDtypeStruct((3 * group, PERIOD), jnp.float32),
                 own,
                 own_mate,
-                visitor,
-                visitor_mate,
+                second,
+                first,
                 kept,
                 backward,
                 twiddle,
@@ -415,24 +426,25 @@
         )
     stack = jnp.stack(stacks)
 
-    step = 2
-    while True:
-        arrived = lax.ppermute(stack, "win", [(w, w ^ step) for w in range(windows)])
-        step *= 2
-        if step == windows:
-            break
+    def from_window(array, flip):
+        return lax.ppermute(array, "win", [(w, w ^ flip) for w in range(windows)])
+
+    for step in (1 << i for i in range(2, windows.bit_length() - 1)):
         stack = call(
-            add_kernel, jax.ShapeDtypeStruct(stack.shape, jnp.float32), stack, arrived
+            add_kernel,
+            jax.ShapeDtypeStruct(stack.shape, jnp.float32),
+            stack,
+            from_window(stack, step),
         )
     result = call(
         result_kernel,
         jax.ShapeDtypeStruct((offsets, group, PERIOD), jnp.float32),
-        stack,
-        arrived,
+        from_window(stack, 1),
+        from_window(stack, 3),
         square,
     )
     return call(
-        join_kernel,
+        functools.partial(join_kernel, blocks),
         jax.ShapeDtypeStruct((1, 2 * offsets, channels, channels, LAGS), jnp.float32),
         result,
         to_mate(result),

time: 16.4 us -> 16.3 us (level)
  waiting for transfers between devices: 5.84 us -> 5.57 us
  starting transfers between devices: 7.24 us -> 7.41 us
    ppermute x1 -> x2, waiting for transfers between devices: 2.6 us -> 1.77 us  [from_window(): return lax.ppermute(array, 'win', [(w, w ^ flip) for w in range(windows)])]
    ppermute x2, waiting for transfers between devices: 2.4 us -> 2.95 us  [from_block(): return lax.ppermute(array, ('chan', 'win'), moves)]
    ppermute x2, starting transfers between devices: 5.16 us -> 4.62 us  [from_block(): return lax.ppermute(array, ('chan', 'win'), moves)]
    ppermute x1 -> x2, starting transfers between devices: 1.55 us -> 2.04 us  [from_window(): return lax.ppermute(array, 'win', [(w, w ^ flip) for w in range(windows)])]
    ppermute x2, starting transfers between devices: 0.52 us -> 0.76 us  [to_mate(): return lax.ppermute(array, 'win', [(w, w ^ 1) for w in range(windows)])]
  transfers between devices with their start and end apart: 5 -> 6, of which waited for: 4 -> 4; matrix products, arithmetic and copies ran while one was open for 0% -> 0% of each run, Pallas kernels for 0% -> 0%
where the time goes in v5:
time: 16.3 us; the launch traced here: 16.2 us
  starting transfers between devices  7.41 us (45%)
  waiting for transfers between devices  5.57 us (34%)
  Pallas kernels  3.16 us (19%)
    ppermute x2, starting transfers between devices, from_block(): return lax.ppermute(array, ('chan', 'win'), moves)  4.62 us
    pallas_call x4, Pallas kernels, call(): pl.pallas_call(kernel, out_shape=out, in_specs=[VMEM] * len(args) if spec...  3.16 us
    ppermute x2, waiting for transfers between devices, from_block(): return lax.ppermute(array, ('chan', 'win'), moves)  2.95 us
    ppermute x2, starting transfers between devices, from_window(): return lax.ppermute(array, 'win', [(w, w ^ flip) for w in range(windows)])  2.04 us
    ppermute x2, waiting for transfers between devices, from_window(): return lax.ppermute(array, 'win', [(w, w ^ flip) for w in range(windows)])  1.77 us
    ppermute x2, waiting for transfers between devices, to_mate(): return lax.ppermute(array, 'win', [(w, w ^ 1) for w in range(windows)])  0.84 us
    ppermute x2, starting transfers between devices, to_mate(): return lax.ppermute(array, 'win', [(w, w ^ 1) for w in range(windows)])  0.76 us
  transfers between devices with their start and end apart: 6, of which 4 were waited for; matrix products, arithmetic and copies ran while one was open for 0% of the time, Pallas kernels for 0%

profile of v5, /device:TPU:0, one launch (start us, length us, event | category | flops | bytes accessed | tf_op | source)
XLA Modules:
  0.0 16.2 jit_solution(6531683649688502832)
XLA Ops:
  0.0 1.8 %shard_map.64 = (bf16[24,1024]{1,0:T(8,128)(2,1)S(1)}, f32[96,128]{1,0:T(8,128)S(1)}, f32[8,128]{1,0:T(8,128)S(1)}, bf16[256,1024]{1,0:T(8,128)(2,1)S(1)}, f32[8,512]{1,0:T(8,128)S(1)}) custom-call(f32[384,128]{1,0:T(8,128)} %bitcast.5, bf16[256,384]{1,0:T(8,128)(2,1)} %constant.10.clone.table_hbm, f32[16,256]{1,0:T(8,128)} %constant.8.clone.twiddle_hbm, ...), custom_call_target="tpu_custom_call" | custom-call | tf_op jit(solution)/shard_map/pallas_call | solution.py:345
  1.8 4.1 %collective-permute-start.2 = (bf16[24,1024]{1,0:T(8,128)(2,1)S(1)}, bf16[24,1024]{1,0:T(8,128)(2,1)S(1)}, u32[]{:S(2)}, u32[]{:S(2)}) collective-permute-start(bf16[24,1024]{1,0:T(8,128)(2,1)S(1)} %get-tuple-element.10.own_ref), channel_id=1, source_target_pairs={{4,0},{8,1},{6,2},{10,3},{9,4},{13,5},{11,6},{15,7},{0,8},{12,9},{... | collective-permute-start | bytes 147464 | tf_op jit(solution)/shard_map/ppermute | solution.py:398
  5.9 0.5 %collective-permute-start.1 = (bf16[24,1024]{1,0:T(8,128)(2,1)S(1)}, bf16[24,1024]{1,0:T(8,128)(2,1)S(1)}, u32[]{:S(2)}, u32[]{:S(2)}) collective-permute-start(bf16[24,1024]{1,0:T(8,128)(2,1)S(1)} %get-tuple-element.10.own_ref), channel_id=1, source_target_pairs={{5,0},{9,1},{7,2},{11,3},{8,4},{12,5},{10,6},{14,7},{1,8},{13,9},{... | collective-permute-start | bytes 147464 | tf_op jit(solution)/shard_map/ppermute | solution.py:398
  6.4 0.0 collective-permute-start
  6.5 1.6 %collective-permute-done.2.first_ref = bf16[24,1024]{1,0:T(8,128)(2,1)S(1)} collective-permute-done((bf16[24,1024]{1,0:T(8,128)(2,1)S(1)}, bf16[24,1024]{1,0:T(8,128)(2,1)S(1)}, u32[]{:S(2)}, u32[]{:S(2)}) %collective-permute-start.2) | collective-permute-done | bytes 49184 | tf_op jit(solution)/shard_map/ppermute | solution.py:398
  8.1 1.3 %collective-permute-done.1.second_ref = bf16[24,1024]{1,0:T(8,128)(2,1)S(1)} collective-permute-done((bf16[24,1024]{1,0:T(8,128)(2,1)S(1)}, bf16[24,1024]{1,0:T(8,128)(2,1)S(1)}, u32[]{:S(2)}, u32[]{:S(2)}) %collective-permute-start.1) | collective-permute-done | bytes 49184 | tf_op jit(solution)/shard_map/ppermute | solution.py:398
  9.4 0.0 collective-permute-done.own_mate_ref
  9.4 0.7 %shard_map.65 = f32[24,512]{1,0:T(8,128)S(1)} custom-call(bf16[24,1024]{1,0:T(8,128)(2,1)S(1)} %get-tuple-element.10.own_ref, bf16[24,1024]{1,0:T(8,128)(2,1)S(1)} %collective-permute-done.own_mate_ref, bf16[24,1024]{1,0:T(8,128)(2,1)S(1)} %collective-permute-done.1.second_ref, bf16[24,1024]{1,0:T(8,128)(2,1)S(1)} %collective-permute-done.2.first_ref, ...), custom_call_target="tpu_custom_call" | custom-call | tf_op jit(solution)/shard_map/pallas_call | solution.py:345
  10.2 2.0 %collective-permute-start.4 = (f32[1,24,512]{2,1,0:T(8,128)S(1)}, f32[1,24,512]{2,1,0:T(8,128)S(1)}, u32[]{:S(2)}, u32[]{:S(2)}) collective-permute-start(f32[1,24,512]{2,1,0:T(8,128)S(1)} %bitcast.3), channel_id=1, source_target_pairs={{0,3},{1,2},{2,1},{3,0},{4,7},{5,6},{6,5},{7,4},{8,11},{9,10},{10,... | collective-permute-start | bytes 147464 | tf_op jit(solution)/shard_map/ppermute | solution.py:430
  12.2 0.0 collective-permute-start.3
  12.2 1.8 %collective-permute-done.4.right_ref = f32[1,24,512]{2,1,0:T(8,128)S(1)} collective-permute-done((f32[1,24,512]{2,1,0:T(8,128)S(1)}, f32[1,24,512]{2,1,0:T(8,128)S(1)}, u32[]{:S(2)}, u32[]{:S(2)}) %collective-permute-start.4) | collective-permute-done | bytes 49184 | tf_op jit(solution)/shard_map/ppermute | solution.py:430
  14.0 0.0 collective-permute-done.3.left_ref
  14.0 0.7 %collective-permute-start.5 = (f32[1,8,512]{2,1,0:T(8,128)S(1)}, f32[1,8,512]{2,1,0:T(8,128)S(1)}, u32[]{:S(2)}, u32[]{:S(2)}) collective-permute-start(f32[1,8,512]{2,1,0:T(8,128)S(1)} %shard_map.66.own_ref), channel_id=1, source_target_pairs={{0,1},{1,0},{2,3},{3,2},{4,5},{5,4},{6,7},{7,6},{8,9},{9,8},{10,11... | collective-permute-start | bytes 49160 | tf_op jit(solution)/shard_map/ppermute | solution.py:389
  14.7 0.8 %collective-permute-done.5.mate_ref = f32[1,8,512]{2,1,0:T(8,128)S(1)} collective-permute-done((f32[1,8,512]{2,1,0:T(8,128)S(1)}, f32[1,8,512]{2,1,0:T(8,128)S(1)}, u32[]{:S(2)}, u32[]{:S(2)}) %collective-permute-start.5) | collective-permute-done | bytes 16416 | tf_op jit(solution)/shard_map/ppermute | solution.py:389
  15.5 0.6 %shard_map.67 = f32[1,2,2,2,1024]{4,3,2,1,0:T(2,128)} custom-call(f32[1,8,512]{2,1,0:T(8,128)S(1)} %shard_map.66.own_ref, f32[1,8,512]{2,1,0:T(8,128)S(1)} %collective-permute-done.5.mate_ref), custom_call_target="tpu_custom_call" | custom-call | tf_op jit(solution)/shard_map/pallas_call | solution.py:345
  (1 shorter events, 0.0 us)
Async XLA Ops:
  1.8 6.3 %collective-permute-start.2 = (bf16[24,1024]{1,0:T(8,128)(2,1)S(1)}, bf16[24,1024]{1,0:T(8,128)(2,1)S(1)}, u32[]{:S(2)}, u32[]{:S(2)}) collective-permute-start(bf16[24,1024]{1,0:T(8,128)(2,1)S(1)} %get-tuple-element.10.own_ref), channel_id=1, source_target_pairs={{4,0},{8,1},{6,2},{10,3},{9,4},{13,5},{11,6},{15,7},{0,8},{12,9},{... | collective-permute-start | bytes 147464 | tf_op jit(solution)/shard_map/ppermute | solution.py:398
  5.9 3.5 %collective-permute-start.1 = (bf16[24,1024]{1,0:T(8,128)(2,1)S(1)}, bf16[24,1024]{1,0:T(8,128)(2,1)S(1)}, u32[]{:S(2)}, u32[]{:S(2)}) collective-permute-start(bf16[24,1024]{1,0:T(8,128)(2,1)S(1)} %get-tuple-element.10.own_ref), channel_id=1, source_target_pairs={{5,0},{9,1},{7,2},{11,3},{8,4},{12,5},{10,6},{14,7},{1,8},{13,9},{... | collective-permute-start | bytes 147464 | tf_op jit(solution)/shard_map/ppermute | solution.py:398
  6.4 3.0 %collective-permute-start = (bf16[24,1024]{1,0:T(8,128)(2,1)S(1)}, bf16[24,1024]{1,0:T(8,128)(2,1)S(1)}, u32[]{:S(2)}, u32[]{:S(2)}) collective-permute-start(bf16[24,1024]{1,0:T(8,128)(2,1)S(1)} %get-tuple-element.10.own_ref), channel_id=1, source_target_pairs={{0,1},{1,0},{2,3},{3,2},{4,5},{5,4},{6,7},{7,6},{8,9},{9,8},{10,11... | collective-permute-start | bytes 147464 | tf_op jit(solution)/shard_map/ppermute | solution.py:389
  10.2 3.8 %collective-permute-start.4 = (f32[1,24,512]{2,1,0:T(8,128)S(1)}, f32[1,24,512]{2,1,0:T(8,128)S(1)}, u32[]{:S(2)}, u32[]{:S(2)}) collective-permute-start(f32[1,24,512]{2,1,0:T(8,128)S(1)} %bitcast.3), channel_id=1, source_target_pairs={{0,3},{1,2},{2,1},{3,0},{4,7},{5,6},{6,5},{7,4},{8,11},{9,10},{10,... | collective-permute-start | bytes 147464 | tf_op jit(solution)/shard_map/ppermute | solution.py:430
  12.2 1.8 %collective-permute-start.3 = (f32[1,24,512]{2,1,0:T(8,128)S(1)}, f32[1,24,512]{2,1,0:T(8,128)S(1)}, u32[]{:S(2)}, u32[]{:S(2)}) collective-permute-start(f32[1,24,512]{2,1,0:T(8,128)S(1)} %bitcast.4), channel_id=1, source_target_pairs={{0,1},{1,0},{2,3},{3,2},{4,5},{5,4},{6,7},{7,6},{8,9},{9,8},{10,11... | collective-permute-start | bytes 147464 | tf_op jit(solution)/shard_map/ppermute | solution.py:430
  14.0 1.6 %collective-permute-start.5 = (f32[1,8,512]{2,1,0:T(8,128)S(1)}, f32[1,8,512]{2,1,0:T(8,128)S(1)}, u32[]{:S(2)}, u32[]{:S(2)}) collective-permute-start(f32[1,8,512]{2,1,0:T(8,128)S(1)} %shard_map.66.own_ref), channel_id=1, source_target_pairs={{0,1},{1,0},{2,3},{3,2},{4,5},{5,4},{6,7},{7,6},{8,9},{9,8},{10,11... | collective-permute-start | bytes 49160 | tf_op jit(solution)/shard_map/ppermute | solution.py:389

commit v6 on v5

--- a/solution.py
+++ b/solution.py
@@ -111,11 +111,16 @@
     sems,
 ):
     copies = [
-        pltpu.make_async_copy(x_hbm, x_ref, sems.at[0]),
         pltpu.make_async_copy(twiddle_hbm, twiddle_ref, sems.at[1]),
         pltpu.make_async_copy(table_hbm, table, sems.at[2]),
         pltpu.make_async_copy(count_hbm, count_ref, sems.at[3]),
     ]
+    piece = x_ref.shape[0] // 4
+    for i in range(4):
+        at = pl.ds(i * piece, piece)
+        copies.append(
+            pltpu.make_async_copy(x_hbm.at[at], x_ref.at[at], sems.at[6 + i])
+        )
     later = [
         pltpu.make_async_copy(backward_hbm, backward_ref, sems.at[4]),
         pltpu.make_async_copy(backward_twiddle_hbm, backward_twiddle_ref, sems.at[5]),
@@ -192,8 +197,11 @@
         (power[4] + power[5]) + (power[6] + power[7])
     )
     mean = jnp.sum(total, axis=1, keepdims=True) * (0.5 / F)
-    floor = 0.09 * (mean + 1e-06)
-    white = [b * lax.rsqrt(jnp.maximum(p, floor)) for b, p in zip(blocks, power)]
+    most = lax.rsqrt(0.09 * (mean + 1e-06))
+    white = [
+        b * jnp.minimum(lax.rsqrt(jnp.maximum(p, 1e-08)), most)
+        for b, p in zip(blocks, power)
+    ]
     for r in range(RADIX):
         first, second = white[r], white[r + RADIX]
         at = 2 * r * QS
@@ -245,6 +253,8 @@
             value = row if value is None else jnp.where(choice == i, row, value)
         return value
 
+    kept = [kept_ref[k * group : (k + 1) * group] for k in range(segments)]
+
     for r in range(RADIX):
         cross_real, cross_imag = [], []
         at = 2 * r * QS
@@ -253,6 +263,7 @@
             own_im = spread(own, own_of, k, at + QS)
             vis_re = spread(visitor, visitor_of, k, at)
             vis_im = spread(visitor, visitor_of, k, at + QS)
+            vis_re, vis_im = vis_re * kept[k], vis_im * kept[k]
             cross_real.append(own_re * vis_re + own_im * vis_im)
             cross_imag.append(own_im * vis_re - own_re * vis_im)
         at = slice(r * segments * group, (r + 1) * segments * group)
@@ -267,8 +278,6 @@
         )
 
     product(0)
-    kept = [kept_ref[k * group : (k + 1) * group] for k in range(segments)]
-
     for c in range(PERIOD // LANES):
         if c + 1 < PERIOD // LANES:
             product(c + 1)
@@ -293,8 +302,8 @@
             earlier = (re[0] - re2) + (im1 - im3), (im[0] - im2) - (re1 - re3)
             for half, (direct, quadrature) in enumerate((earlier, later)):
                 power = direct * direct + quadrature * quadrature
-                scale = lax.rsqrt(jnp.maximum(power, 0.25)) * kept[k]
-                terms = (direct * kept[k], direct * scale, quadrature * scale)
+                scale = lax.rsqrt(jnp.maximum(power, 0.25))
+                terms = (direct, direct * scale, quadrature * scale)
                 for i, term in enumerate(terms):
                     old = sums[half][i]
                     sums[half][i] = term if old is None else old + term
@@ -381,7 +390,7 @@
         specs=[HBM] * 6,
         scratch=(
             *(pltpu.VMEM(x.shape, x.dtype) for x in inputs),
-            pltpu.SemaphoreType.DMA((6,)),
+            pltpu.SemaphoreType.DMA((10,)),
         ),
     )
 

time: 16.3 us -> 16.4 us (level)
  no operation moved by 1% of the time
where the time goes in v6:
time: 16.4 us; the launch traced here: 16.1 us
  starting transfers between devices  7.43 us (45%)
  waiting for transfers between devices  5.56 us (34%)
  Pallas kernels  3.11 us (19%)
    ppermute x2, starting transfers between devices, from_block(): return lax.ppermute(array, ('chan', 'win'), moves)  4.62 us
    pallas_call x4, Pallas kernels, call(): pl.pallas_call(kernel, out_shape=out, in_specs=[VMEM] * len(args) if spec...  3.11 us
    ppermute x2, waiting for transfers between devices, from_block(): return lax.ppermute(array, ('chan', 'win'), moves)  2.95 us
    ppermute x2, starting transfers between devices, from_window(): return lax.ppermute(array, 'win', [(w, w ^ flip) for w in range(windows)])  2.05 us
    ppermute x2, waiting for transfers between devices, from_window(): return lax.ppermute(array, 'win', [(w, w ^ flip) for w in range(windows)])  1.77 us
    ppermute x2, waiting for transfers between devices, to_mate(): return lax.ppermute(array, 'win', [(w, w ^ 1) for w in range(windows)])  0.84 us
    ppermute x2, starting transfers between devices, to_mate(): return lax.ppermute(array, 'win', [(w, w ^ 1) for w in range(windows)])  0.75 us
  transfers between devices with their start and end apart: 6, of which 4 were waited for; matrix products, arithmetic and copies ran while one was open for 0% of the time, Pallas kernels for 0%

profile of v6, /device:TPU:0, one launch (start us, length us, event | category | flops | bytes accessed | tf_op | source)
XLA Modules:
  0.0 16.1 jit_solution(3419161371962785284)
XLA Ops:
  0.0 1.8 %shard_map.64 = (bf16[24,1024]{1,0:T(8,128)(2,1)S(1)}, f32[96,128]{1,0:T(8,128)S(1)}, f32[8,128]{1,0:T(8,128)S(1)}, bf16[256,1024]{1,0:T(8,128)(2,1)S(1)}, f32[8,512]{1,0:T(8,128)S(1)}) custom-call(f32[384,128]{1,0:T(8,128)} %bitcast.5, bf16[256,384]{1,0:T(8,128)(2,1)} %constant.10.clone.table_hbm, f32[16,256]{1,0:T(8,128)} %constant.8.clone.twiddle_hbm, ...), custom_call_target="tpu_custom_call" | custom-call | tf_op jit(solution)/shard_map/pallas_call | solution.py:354
  1.8 4.1 %collective-permute-start.2 = (bf16[24,1024]{1,0:T(8,128)(2,1)S(1)}, bf16[24,1024]{1,0:T(8,128)(2,1)S(1)}, u32[]{:S(2)}, u32[]{:S(2)}) collective-permute-start(bf16[24,1024]{1,0:T(8,128)(2,1)S(1)} %get-tuple-element.10.own_ref), channel_id=1, source_target_pairs={{4,0},{8,1},{6,2},{10,3},{9,4},{13,5},{11,6},{15,7},{0,8},{12,9},{... | collective-permute-start | bytes 147464 | tf_op jit(solution)/shard_map/ppermute | solution.py:407
  5.9 0.5 %collective-permute-start.1 = (bf16[24,1024]{1,0:T(8,128)(2,1)S(1)}, bf16[24,1024]{1,0:T(8,128)(2,1)S(1)}, u32[]{:S(2)}, u32[]{:S(2)}) collective-permute-start(bf16[24,1024]{1,0:T(8,128)(2,1)S(1)} %get-tuple-element.10.own_ref), channel_id=1, source_target_pairs={{5,0},{9,1},{7,2},{11,3},{8,4},{12,5},{10,6},{14,7},{1,8},{13,9},{... | collective-permute-start | bytes 147464 | tf_op jit(solution)/shard_map/ppermute | solution.py:407
  6.4 0.0 collective-permute-start
  6.5 1.6 %collective-permute-done.2.first_ref = bf16[24,1024]{1,0:T(8,128)(2,1)S(1)} collective-permute-done((bf16[24,1024]{1,0:T(8,128)(2,1)S(1)}, bf16[24,1024]{1,0:T(8,128)(2,1)S(1)}, u32[]{:S(2)}, u32[]{:S(2)}) %collective-permute-start.2) | collective-permute-done | bytes 49184 | tf_op jit(solution)/shard_map/ppermute | solution.py:407
  8.1 1.3 %collective-permute-done.1.second_ref = bf16[24,1024]{1,0:T(8,128)(2,1)S(1)} collective-permute-done((bf16[24,1024]{1,0:T(8,128)(2,1)S(1)}, bf16[24,1024]{1,0:T(8,128)(2,1)S(1)}, u32[]{:S(2)}, u32[]{:S(2)}) %collective-permute-start.1) | collective-permute-done | bytes 49184 | tf_op jit(solution)/shard_map/ppermute | solution.py:407
  9.4 0.0 collective-permute-done.own_mate_ref
  9.4 0.7 %shard_map.65 = f32[24,512]{1,0:T(8,128)S(1)} custom-call(bf16[24,1024]{1,0:T(8,128)(2,1)S(1)} %get-tuple-element.10.own_ref, bf16[24,1024]{1,0:T(8,128)(2,1)S(1)} %collective-permute-done.own_mate_ref, bf16[24,1024]{1,0:T(8,128)(2,1)S(1)} %collective-permute-done.1.second_ref, bf16[24,1024]{1,0:T(8,128)(2,1)S(1)} %collective-permute-done.2.first_ref, ...), custom_call_target="tpu_custom_call" | custom-call | tf_op jit(solution)/shard_map/pallas_call | solution.py:354
  10.1 2.0 %collective-permute-start.4 = (f32[1,24,512]{2,1,0:T(8,128)S(1)}, f32[1,24,512]{2,1,0:T(8,128)S(1)}, u32[]{:S(2)}, u32[]{:S(2)}) collective-permute-start(f32[1,24,512]{2,1,0:T(8,128)S(1)} %bitcast.3), channel_id=1, source_target_pairs={{0,3},{1,2},{2,1},{3,0},{4,7},{5,6},{6,5},{7,4},{8,11},{9,10},{10,... | collective-permute-start | bytes 147464 | tf_op jit(solution)/shard_map/ppermute | solution.py:439
  12.2 0.0 collective-permute-start.3
  12.2 1.8 %collective-permute-done.4.right_ref = f32[1,24,512]{2,1,0:T(8,128)S(1)} collective-permute-done((f32[1,24,512]{2,1,0:T(8,128)S(1)}, f32[1,24,512]{2,1,0:T(8,128)S(1)}, u32[]{:S(2)}, u32[]{:S(2)}) %collective-permute-start.4) | collective-permute-done | bytes 49184 | tf_op jit(solution)/shard_map/ppermute | solution.py:439
  13.9 0.0 collective-permute-done.3.left_ref
  14.0 0.7 %collective-permute-start.5 = (f32[1,8,512]{2,1,0:T(8,128)S(1)}, f32[1,8,512]{2,1,0:T(8,128)S(1)}, u32[]{:S(2)}, u32[]{:S(2)}) collective-permute-start(f32[1,8,512]{2,1,0:T(8,128)S(1)} %shard_map.66.own_ref), channel_id=1, source_target_pairs={{0,1},{1,0},{2,3},{3,2},{4,5},{5,4},{6,7},{7,6},{8,9},{9,8},{10,11... | collective-permute-start | bytes 49160 | tf_op jit(solution)/shard_map/ppermute | solution.py:398
  14.7 0.8 %collective-permute-done.5.mate_ref = f32[1,8,512]{2,1,0:T(8,128)S(1)} collective-permute-done((f32[1,8,512]{2,1,0:T(8,128)S(1)}, f32[1,8,512]{2,1,0:T(8,128)S(1)}, u32[]{:S(2)}, u32[]{:S(2)}) %collective-permute-start.5) | collective-permute-done | bytes 16416 | tf_op jit(solution)/shard_map/ppermute | solution.py:398
  15.5 0.6 %shard_map.67 = f32[1,2,2,2,1024]{4,3,2,1,0:T(2,128)} custom-call(f32[1,8,512]{2,1,0:T(8,128)S(1)} %shard_map.66.own_ref, f32[1,8,512]{2,1,0:T(8,128)S(1)} %collective-permute-done.5.mate_ref), custom_call_target="tpu_custom_call" | custom-call | tf_op jit(solution)/shard_map/pallas_call | solution.py:354
  (1 shorter events, 0.0 us)
Async XLA Ops:
  1.8 6.3 %collective-permute-start.2 = (bf16[24,1024]{1,0:T(8,128)(2,1)S(1)}, bf16[24,1024]{1,0:T(8,128)(2,1)S(1)}, u32[]{:S(2)}, u32[]{:S(2)}) collective-permute-start(bf16[24,1024]{1,0:T(8,128)(2,1)S(1)} %get-tuple-element.10.own_ref), channel_id=1, source_target_pairs={{4,0},{8,1},{6,2},{10,3},{9,4},{13,5},{11,6},{15,7},{0,8},{12,9},{... | collective-permute-start | bytes 147464 | tf_op jit(solution)/shard_map/ppermute | solution.py:407
  5.9 3.5 %collective-permute-start.1 = (bf16[24,1024]{1,0:T(8,128)(2,1)S(1)}, bf16[24,1024]{1,0:T(8,128)(2,1)S(1)}, u32[]{:S(2)}, u32[]{:S(2)}) collective-permute-start(bf16[24,1024]{1,0:T(8,128)(2,1)S(1)} %get-tuple-element.10.own_ref), channel_id=1, source_target_pairs={{5,0},{9,1},{7,2},{11,3},{8,4},{12,5},{10,6},{14,7},{1,8},{13,9},{... | collective-permute-start | bytes 147464 | tf_op jit(solution)/shard_map/ppermute | solution.py:407
  6.4 3.0 %collective-permute-start = (bf16[24,1024]{1,0:T(8,128)(2,1)S(1)}, bf16[24,1024]{1,0:T(8,128)(2,1)S(1)}, u32[]{:S(2)}, u32[]{:S(2)}) collective-permute-start(bf16[24,1024]{1,0:T(8,128)(2,1)S(1)} %get-tuple-element.10.own_ref), channel_id=1, source_target_pairs={{0,1},{1,0},{2,3},{3,2},{4,5},{5,4},{6,7},{7,6},{8,9},{9,8},{10,11... | collective-permute-start | bytes 147464 | tf_op jit(solution)/shard_map/ppermute | solution.py:398
  10.1 3.8 %collective-permute-start.4 = (f32[1,24,512]{2,1,0:T(8,128)S(1)}, f32[1,24,512]{2,1,0:T(8,128)S(1)}, u32[]{:S(2)}, u32[]{:S(2)}) collective-permute-start(f32[1,24,512]{2,1,0:T(8,128)S(1)} %bitcast.3), channel_id=1, source_target_pairs={{0,3},{1,2},{2,1},{3,0},{4,7},{5,6},{6,5},{7,4},{8,11},{9,10},{10,... | collective-permute-start | bytes 147464 | tf_op jit(solution)/shard_map/ppermute | solution.py:439
  12.2 1.8 %collective-permute-start.3 = (f32[1,24,512]{2,1,0:T(8,128)S(1)}, f32[1,24,512]{2,1,0:T(8,128)S(1)}, u32[]{:S(2)}, u32[]{:S(2)}) collective-permute-start(f32[1,24,512]{2,1,0:T(8,128)S(1)} %bitcast.4), channel_id=1, source_target_pairs={{0,1},{1,0},{2,3},{3,2},{4,5},{5,4},{6,7},{7,6},{8,9},{9,8},{10,11... | collective-permute-start | bytes 147464 | tf_op jit(solution)/shard_map/ppermute | solution.py:439
  14.0 1.5 %collective-permute-start.5 = (f32[1,8,512]{2,1,0:T(8,128)S(1)}, f32[1,8,512]{2,1,0:T(8,128)S(1)}, u32[]{:S(2)}, u32[]{:S(2)}) collective-permute-start(f32[1,8,512]{2,1,0:T(8,128)S(1)} %shard_map.66.own_ref), channel_id=1, source_target_pairs={{0,1},{1,0},{2,3},{3,2},{4,5},{5,4},{6,7},{7,6},{8,9},{9,8},{10,11... | collective-permute-start | bytes 49160 | tf_op jit(solution)/shard_map/ppermute | solution.py:398

commit v7 on v6

--- a/solution.py
+++ b/solution.py
@@ -269,6 +269,11 @@
         at = slice(r * segments * group, (r + 1) * segments * group)
         cross[at, 0:QS] = jnp.concatenate(cross_real, axis=0).astype(jnp.bfloat16)
         cross[at, QS:] = jnp.concatenate(cross_imag, axis=0).astype(jnp.bfloat16)
+        inner[0, at] = jnp.dot(
+            cross[at],
+            table_ref[:, : 2 * LANES],
+            preferred_element_type=jnp.float32,
+        )
 
     def product(c):
         inner[c] = jnp.dot(
@@ -277,7 +282,6 @@
             preferred_element_type=jnp.float32,
         )
 
-    product(0)
     for c in range(PERIOD // LANES):
         if c + 1 < PERIOD // LANES:
             product(c + 1)

time: 16.4 us -> 16.4 us (level)
  no operation moved by 1% of the time
where the time goes in v7:
time: 16.4 us; the launch traced here: 16.1 us
  starting transfers between devices  7.42 us (45%)
  waiting for transfers between devices  5.56 us (34%)
  Pallas kernels  3.12 us (19%)
    ppermute x2, starting transfers between devices, from_block(): return lax.ppermute(array, ('chan', 'win'), moves)  4.62 us
    pallas_call x4, Pallas kernels, call(): pl.pallas_call(kernel, out_shape=out, in_specs=[VMEM] * len(args) if spec...  3.12 us
    ppermute x2, waiting for transfers between devices, from_block(): return lax.ppermute(array, ('chan', 'win'), moves)  2.95 us
    ppermute x2, starting transfers between devices, from_window(): return lax.ppermute(array, 'win', [(w, w ^ flip) for w in range(windows)])  2.06 us
    ppermute x2, waiting for transfers between devices, from_window(): return lax.ppermute(array, 'win', [(w, w ^ flip) for w in range(windows)])  1.77 us
    ppermute x2, waiting for transfers between devices, to_mate(): return lax.ppermute(array, 'win', [(w, w ^ 1) for w in range(windows)])  0.84 us
    ppermute x2, starting transfers between devices, to_mate(): return lax.ppermute(array, 'win', [(w, w ^ 1) for w in range(windows)])  0.74 us
  transfers between devices with their start and end apart: 6, of which 4 were waited for; matrix products, arithmetic and copies ran while one was open for 0% of the time, Pallas kernels for 0%

profile of v7, /device:TPU:0, one launch (start us, length us, event | category | flops | bytes accessed | tf_op | source)
XLA Modules:
  0.0 16.1 jit_solution(11402459560983289713)
XLA Ops:
  0.0 1.8 %shard_map.64 = (bf16[24,1024]{1,0:T(8,128)(2,1)S(1)}, f32[96,128]{1,0:T(8,128)S(1)}, f32[8,128]{1,0:T(8,128)S(1)}, bf16[256,1024]{1,0:T(8,128)(2,1)S(1)}, f32[8,512]{1,0:T(8,128)S(1)}) custom-call(f32[384,128]{1,0:T(8,128)} %bitcast.5, bf16[256,384]{1,0:T(8,128)(2,1)} %constant.10.clone.table_hbm, f32[16,256]{1,0:T(8,128)} %constant.8.clone.twiddle_hbm, ...), custom_call_target="tpu_custom_call" | custom-call | tf_op jit(solution)/shard_map/pallas_call | solution.py:358
  1.8 4.1 %collective-permute-start.2 = (bf16[24,1024]{1,0:T(8,128)(2,1)S(1)}, bf16[24,1024]{1,0:T(8,128)(2,1)S(1)}, u32[]{:S(2)}, u32[]{:S(2)}) collective-permute-start(bf16[24,1024]{1,0:T(8,128)(2,1)S(1)} %get-tuple-element.10.own_ref), channel_id=1, source_target_pairs={{4,0},{8,1},{6,2},{10,3},{9,4},{13,5},{11,6},{15,7},{0,8},{12,9},{... | collective-permute-start | bytes 147464 | tf_op jit(solution)/shard_map/ppermute | solution.py:411
  5.9 0.5 %collective-permute-start.1 = (bf16[24,1024]{1,0:T(8,128)(2,1)S(1)}, bf16[24,1024]{1,0:T(8,128)(2,1)S(1)}, u32[]{:S(2)}, u32[]{:S(2)}) collective-permute-start(bf16[24,1024]{1,0:T(8,128)(2,1)S(1)} %get-tuple-element.10.own_ref), channel_id=1, source_target_pairs={{5,0},{9,1},{7,2},{11,3},{8,4},{12,5},{10,6},{14,7},{1,8},{13,9},{... | collective-permute-start | bytes 147464 | tf_op jit(solution)/shard_map/ppermute | solution.py:411
  6.4 0.0 collective-permute-start
  6.5 1.6 %collective-permute-done.2.first_ref = bf16[24,1024]{1,0:T(8,128)(2,1)S(1)} collective-permute-done((bf16[24,1024]{1,0:T(8,128)(2,1)S(1)}, bf16[24,1024]{1,0:T(8,128)(2,1)S(1)}, u32[]{:S(2)}, u32[]{:S(2)}) %collective-permute-start.2) | collective-permute-done | bytes 49184 | tf_op jit(solution)/shard_map/ppermute | solution.py:411
  8.1 1.3 %collective-permute-done.1.second_ref = bf16[24,1024]{1,0:T(8,128)(2,1)S(1)} collective-permute-done((bf16[24,1024]{1,0:T(8,128)(2,1)S(1)}, bf16[24,1024]{1,0:T(8,128)(2,1)S(1)}, u32[]{:S(2)}, u32[]{:S(2)}) %collective-permute-start.1) | collective-permute-done | bytes 49184 | tf_op jit(solution)/shard_map/ppermute | solution.py:411
  9.4 0.0 collective-permute-done.own_mate_ref
  9.4 0.7 %shard_map.65 = f32[24,512]{1,0:T(8,128)S(1)} custom-call(bf16[24,1024]{1,0:T(8,128)(2,1)S(1)} %get-tuple-element.10.own_ref, bf16[24,1024]{1,0:T(8,128)(2,1)S(1)} %collective-permute-done.own_mate_ref, bf16[24,1024]{1,0:T(8,128)(2,1)S(1)} %collective-permute-done.1.second_ref, bf16[24,1024]{1,0:T(8,128)(2,1)S(1)} %collective-permute-done.2.first_ref, ...), custom_call_target="tpu_custom_call" | custom-call | tf_op jit(solution)/shard_map/pallas_call | solution.py:358
  10.1 2.1 %collective-permute-start.4 = (f32[1,24,512]{2,1,0:T(8,128)S(1)}, f32[1,24,512]{2,1,0:T(8,128)S(1)}, u32[]{:S(2)}, u32[]{:S(2)}) collective-permute-start(f32[1,24,512]{2,1,0:T(8,128)S(1)} %bitcast.3), channel_id=1, source_target_pairs={{0,3},{1,2},{2,1},{3,0},{4,7},{5,6},{6,5},{7,4},{8,11},{9,10},{10,... | collective-permute-start | bytes 147464 | tf_op jit(solution)/shard_map/ppermute | solution.py:443
  12.2 0.0 collective-permute-start.3
  12.2 1.8 %collective-permute-done.4.right_ref = f32[1,24,512]{2,1,0:T(8,128)S(1)} collective-permute-done((f32[1,24,512]{2,1,0:T(8,128)S(1)}, f32[1,24,512]{2,1,0:T(8,128)S(1)}, u32[]{:S(2)}, u32[]{:S(2)}) %collective-permute-start.4) | collective-permute-done | bytes 49184 | tf_op jit(solution)/shard_map/ppermute | solution.py:443
  14.0 0.0 collective-permute-done.3.left_ref
  14.0 0.7 %collective-permute-start.5 = (f32[1,8,512]{2,1,0:T(8,128)S(1)}, f32[1,8,512]{2,1,0:T(8,128)S(1)}, u32[]{:S(2)}, u32[]{:S(2)}) collective-permute-start(f32[1,8,512]{2,1,0:T(8,128)S(1)} %shard_map.66.own_ref), channel_id=1, source_target_pairs={{0,1},{1,0},{2,3},{3,2},{4,5},{5,4},{6,7},{7,6},{8,9},{9,8},{10,11... | collective-permute-start | bytes 49160 | tf_op jit(solution)/shard_map/ppermute | solution.py:402
  14.7 0.8 %collective-permute-done.5.mate_ref = f32[1,8,512]{2,1,0:T(8,128)S(1)} collective-permute-done((f32[1,8,512]{2,1,0:T(8,128)S(1)}, f32[1,8,512]{2,1,0:T(8,128)S(1)}, u32[]{:S(2)}, u32[]{:S(2)}) %collective-permute-start.5) | collective-permute-done | bytes 16416 | tf_op jit(solution)/shard_map/ppermute | solution.py:402
  15.5 0.6 %shard_map.67 = f32[1,2,2,2,1024]{4,3,2,1,0:T(2,128)} custom-call(f32[1,8,512]{2,1,0:T(8,128)S(1)} %shard_map.66.own_ref, f32[1,8,512]{2,1,0:T(8,128)S(1)} %collective-permute-done.5.mate_ref), custom_call_target="tpu_custom_call" | custom-call | tf_op jit(solution)/shard_map/pallas_call | solution.py:358
  (1 shorter events, 0.0 us)
Async XLA Ops:
  1.8 6.3 %collective-permute-start.2 = (bf16[24,1024]{1,0:T(8,128)(2,1)S(1)}, bf16[24,1024]{1,0:T(8,128)(2,1)S(1)}, u32[]{:S(2)}, u32[]{:S(2)}) collective-permute-start(bf16[24,1024]{1,0:T(8,128)(2,1)S(1)} %get-tuple-element.10.own_ref), channel_id=1, source_target_pairs={{4,0},{8,1},{6,2},{10,3},{9,4},{13,5},{11,6},{15,7},{0,8},{12,9},{... | collective-permute-start | bytes 147464 | tf_op jit(solution)/shard_map/ppermute | solution.py:411
  5.9 3.5 %collective-permute-start.1 = (bf16[24,1024]{1,0:T(8,128)(2,1)S(1)}, bf16[24,1024]{1,0:T(8,128)(2,1)S(1)}, u32[]{:S(2)}, u32[]{:S(2)}) collective-permute-start(bf16[24,1024]{1,0:T(8,128)(2,1)S(1)} %get-tuple-element.10.own_ref), channel_id=1, source_target_pairs={{5,0},{9,1},{7,2},{11,3},{8,4},{12,5},{10,6},{14,7},{1,8},{13,9},{... | collective-permute-start | bytes 147464 | tf_op jit(solution)/shard_map/ppermute | solution.py:411
  6.4 3.0 %collective-permute-start = (bf16[24,1024]{1,0:T(8,128)(2,1)S(1)}, bf16[24,1024]{1,0:T(8,128)(2,1)S(1)}, u32[]{:S(2)}, u32[]{:S(2)}) collective-permute-start(bf16[24,1024]{1,0:T(8,128)(2,1)S(1)} %get-tuple-element.10.own_ref), channel_id=1, source_target_pairs={{0,1},{1,0},{2,3},{3,2},{4,5},{5,4},{6,7},{7,6},{8,9},{9,8},{10,11... | collective-permute-start | bytes 147464 | tf_op jit(solution)/shard_map/ppermute | solution.py:402
  10.1 3.8 %collective-permute-start.4 = (f32[1,24,512]{2,1,0:T(8,128)S(1)}, f32[1,24,512]{2,1,0:T(8,128)S(1)}, u32[]{:S(2)}, u32[]{:S(2)}) collective-permute-start(f32[1,24,512]{2,1,0:T(8,128)S(1)} %bitcast.3), channel_id=1, source_target_pairs={{0,3},{1,2},{2,1},{3,0},{4,7},{5,6},{6,5},{7,4},{8,11},{9,10},{10,... | collective-permute-start | bytes 147464 | tf_op jit(solution)/shard_map/ppermute | solution.py:443
  12.2 1.8 %collective-permute-start.3 = (f32[1,24,512]{2,1,0:T(8,128)S(1)}, f32[1,24,512]{2,1,0:T(8,128)S(1)}, u32[]{:S(2)}, u32[]{:S(2)}) collective-permute-start(f32[1,24,512]{2,1,0:T(8,128)S(1)} %bitcast.4), channel_id=1, source_target_pairs={{0,1},{1,0},{2,3},{3,2},{4,5},{5,4},{6,7},{7,6},{8,9},{9,8},{10,11... | collective-permute-start | bytes 147464 | tf_op jit(solution)/shard_map/ppermute | solution.py:443
  14.0 1.5 %collective-permute-start.5 = (f32[1,8,512]{2,1,0:T(8,128)S(1)}, f32[1,8,512]{2,1,0:T(8,128)S(1)}, u32[]{:S(2)}, u32[]{:S(2)}) collective-permute-start(f32[1,8,512]{2,1,0:T(8,128)S(1)} %shard_map.66.own_ref), channel_id=1, source_target_pairs={{0,1},{1,0},{2,3},{3,2},{4,5},{5,4},{6,7},{7,6},{8,9},{9,8},{10,11... | collective-permute-start | bytes 49160 | tf_op jit(solution)/shard_map/ppermute | solution.py:402

commit v8 on v6

--- a/solution.py
+++ b/solution.py
@@ -125,6 +125,7 @@
         pltpu.make_async_copy(backward_hbm, backward_ref, sems.at[4]),
         pltpu.make_async_copy(backward_twiddle_hbm, backward_twiddle_ref, sems.at[5]),
     ]
+    copies = copies[3:] + copies[:3]
     for copy in copies + later:
         copy.start()
     for copy in copies:

time: 16.4 us -> 16.3 us (level)
  no operation moved by 1% of the time
where the time goes in v8:
time: 16.3 us; the launch traced here: 16.2 us
  starting transfers between devices  7.43 us (46%)
  waiting for transfers between devices  5.56 us (34%)
  Pallas kernels  3.17 us (19%)
    ppermute x2, starting transfers between devices, from_block(): return lax.ppermute(array, ('chan', 'win'), moves)  4.62 us
    pallas_call x4, Pallas kernels, call(): pl.pallas_call(kernel, out_shape=out, in_specs=[VMEM] * len(args) if spec...  3.17 us
    ppermute x2, waiting for transfers between devices, from_block(): return lax.ppermute(array, ('chan', 'win'), moves)  2.95 us
    ppermute x2, starting transfers between devices, from_window(): return lax.ppermute(array, 'win', [(w, w ^ flip) for w in range(windows)])  2.05 us
    ppermute x2, waiting for transfers between devices, from_window(): return lax.ppermute(array, 'win', [(w, w ^ flip) for w in range(windows)])  1.77 us
    ppermute x2, waiting for transfers between devices, to_mate(): return lax.ppermute(array, 'win', [(w, w ^ 1) for w in range(windows)])  0.84 us
    ppermute x2, starting transfers between devices, to_mate(): return lax.ppermute(array, 'win', [(w, w ^ 1) for w in range(windows)])  0.75 us
  transfers between devices with their start and end apart: 6, of which 4 were waited for; matrix products, arithmetic and copies ran while one was open for 0% of the time, Pallas kernels for 0%

profile of v8, /device:TPU:0, one launch (start us, length us, event | category | flops | bytes accessed | tf_op | source)
XLA Modules:
  0.0 16.2 jit_solution(9474661459214969705)
XLA Ops:
  0.0 1.9 %shard_map.64 = (bf16[24,1024]{1,0:T(8,128)(2,1)S(1)}, f32[96,128]{1,0:T(8,128)S(1)}, f32[8,128]{1,0:T(8,128)S(1)}, bf16[256,1024]{1,0:T(8,128)(2,1)S(1)}, f32[8,512]{1,0:T(8,128)S(1)}) custom-call(f32[384,128]{1,0:T(8,128)} %bitcast.5, bf16[256,384]{1,0:T(8,128)(2,1)} %constant.10.clone.table_hbm, f32[16,256]{1,0:T(8,128)} %constant.8.clone.twiddle_hbm, ...), custom_call_target="tpu_custom_call" | custom-call | tf_op jit(solution)/shard_map/pallas_call | solution.py:355
  1.9 4.1 %collective-permute-start.2 = (bf16[24,1024]{1,0:T(8,128)(2,1)S(1)}, bf16[24,1024]{1,0:T(8,128)(2,1)S(1)}, u32[]{:S(2)}, u32[]{:S(2)}) collective-permute-start(bf16[24,1024]{1,0:T(8,128)(2,1)S(1)} %get-tuple-element.10.own_ref), channel_id=1, source_target_pairs={{4,0},{8,1},{6,2},{10,3},{9,4},{13,5},{11,6},{15,7},{0,8},{12,9},{... | collective-permute-start | bytes 147464 | tf_op jit(solution)/shard_map/ppermute | solution.py:408
  6.0 0.5 %collective-permute-start.1 = (bf16[24,1024]{1,0:T(8,128)(2,1)S(1)}, bf16[24,1024]{1,0:T(8,128)(2,1)S(1)}, u32[]{:S(2)}, u32[]{:S(2)}) collective-permute-start(bf16[24,1024]{1,0:T(8,128)(2,1)S(1)} %get-tuple-element.10.own_ref), channel_id=1, source_target_pairs={{5,0},{9,1},{7,2},{11,3},{8,4},{12,5},{10,6},{14,7},{1,8},{13,9},{... | collective-permute-start | bytes 147464 | tf_op jit(solution)/shard_map/ppermute | solution.py:408
  6.5 0.0 collective-permute-start
  6.5 1.6 %collective-permute-done.2.first_ref = bf16[24,1024]{1,0:T(8,128)(2,1)S(1)} collective-permute-done((bf16[24,1024]{1,0:T(8,128)(2,1)S(1)}, bf16[24,1024]{1,0:T(8,128)(2,1)S(1)}, u32[]{:S(2)}, u32[]{:S(2)}) %collective-permute-start.2) | collective-permute-done | bytes 49184 | tf_op jit(solution)/shard_map/ppermute | solution.py:408
  8.1 1.3 %collective-permute-done.1.second_ref = bf16[24,1024]{1,0:T(8,128)(2,1)S(1)} collective-permute-done((bf16[24,1024]{1,0:T(8,128)(2,1)S(1)}, bf16[24,1024]{1,0:T(8,128)(2,1)S(1)}, u32[]{:S(2)}, u32[]{:S(2)}) %collective-permute-start.1) | collective-permute-done | bytes 49184 | tf_op jit(solution)/shard_map/ppermute | solution.py:408
  9.5 0.0 collective-permute-done.own_mate_ref
  9.5 0.7 %shard_map.65 = f32[24,512]{1,0:T(8,128)S(1)} custom-call(bf16[24,1024]{1,0:T(8,128)(2,1)S(1)} %get-tuple-element.10.own_ref, bf16[24,1024]{1,0:T(8,128)(2,1)S(1)} %collective-permute-done.own_mate_ref, bf16[24,1024]{1,0:T(8,128)(2,1)S(1)} %collective-permute-done.1.second_ref, bf16[24,1024]{1,0:T(8,128)(2,1)S(1)} %collective-permute-done.2.first_ref, ...), custom_call_target="tpu_custom_call" | custom-call | tf_op jit(solution)/shard_map/pallas_call | solution.py:355
  10.2 2.0 %collective-permute-start.4 = (f32[1,24,512]{2,1,0:T(8,128)S(1)}, f32[1,24,512]{2,1,0:T(8,128)S(1)}, u32[]{:S(2)}, u32[]{:S(2)}) collective-permute-start(f32[1,24,512]{2,1,0:T(8,128)S(1)} %bitcast.3), channel_id=1, source_target_pairs={{0,3},{1,2},{2,1},{3,0},{4,7},{5,6},{6,5},{7,4},{8,11},{9,10},{10,... | collective-permute-start | bytes 147464 | tf_op jit(solution)/shard_map/ppermute | solution.py:440
  12.2 0.0 collective-permute-start.3
  12.2 1.8 %collective-permute-done.4.right_ref = f32[1,24,512]{2,1,0:T(8,128)S(1)} collective-permute-done((f32[1,24,512]{2,1,0:T(8,128)S(1)}, f32[1,24,512]{2,1,0:T(8,128)S(1)}, u32[]{:S(2)}, u32[]{:S(2)}) %collective-permute-start.4) | collective-permute-done | bytes 49184 | tf_op jit(solution)/shard_map/ppermute | solution.py:440
  14.0 0.0 collective-permute-done.3.left_ref
  14.0 0.7 %collective-permute-start.5 = (f32[1,8,512]{2,1,0:T(8,128)S(1)}, f32[1,8,512]{2,1,0:T(8,128)S(1)}, u32[]{:S(2)}, u32[]{:S(2)}) collective-permute-start(f32[1,8,512]{2,1,0:T(8,128)S(1)} %shard_map.66.own_ref), channel_id=1, source_target_pairs={{0,1},{1,0},{2,3},{3,2},{4,5},{5,4},{6,7},{7,6},{8,9},{9,8},{10,11... | collective-permute-start | bytes 49160 | tf_op jit(solution)/shard_map/ppermute | solution.py:399
  14.7 0.8 %collective-permute-done.5.mate_ref = f32[1,8,512]{2,1,0:T(8,128)S(1)} collective-permute-done((f32[1,8,512]{2,1,0:T(8,128)S(1)}, f32[1,8,512]{2,1,0:T(8,128)S(1)}, u32[]{:S(2)}, u32[]{:S(2)}) %collective-permute-start.5) | collective-permute-done | bytes 16416 | tf_op jit(solution)/shard_map/ppermute | solution.py:399
  15.6 0.6 %shard_map.67 = f32[1,2,2,2,1024]{4,3,2,1,0:T(2,128)} custom-call(f32[1,8,512]{2,1,0:T(8,128)S(1)} %shard_map.66.own_ref, f32[1,8,512]{2,1,0:T(8,128)S(1)} %collective-permute-done.5.mate_ref), custom_call_target="tpu_custom_call" | custom-call | tf_op jit(solution)/shard_map/pallas_call | solution.py:355
  (1 shorter events, 0.0 us)
Async XLA Ops:
  1.9 6.3 %collective-permute-start.2 = (bf16[24,1024]{1,0:T(8,128)(2,1)S(1)}, bf16[24,1024]{1,0:T(8,128)(2,1)S(1)}, u32[]{:S(2)}, u32[]{:S(2)}) collective-permute-start(bf16[24,1024]{1,0:T(8,128)(2,1)S(1)} %get-tuple-element.10.own_ref), channel_id=1, source_target_pairs={{4,0},{8,1},{6,2},{10,3},{9,4},{13,5},{11,6},{15,7},{0,8},{12,9},{... | collective-permute-start | bytes 147464 | tf_op jit(solution)/shard_map/ppermute | solution.py:408
  6.0 3.5 %collective-permute-start.1 = (bf16[24,1024]{1,0:T(8,128)(2,1)S(1)}, bf16[24,1024]{1,0:T(8,128)(2,1)S(1)}, u32[]{:S(2)}, u32[]{:S(2)}) collective-permute-start(bf16[24,1024]{1,0:T(8,128)(2,1)S(1)} %get-tuple-element.10.own_ref), channel_id=1, source_target_pairs={{5,0},{9,1},{7,2},{11,3},{8,4},{12,5},{10,6},{14,7},{1,8},{13,9},{... | collective-permute-start | bytes 147464 | tf_op jit(solution)/shard_map/ppermute | solution.py:408
  6.5 3.0 %collective-permute-start = (bf16[24,1024]{1,0:T(8,128)(2,1)S(1)}, bf16[24,1024]{1,0:T(8,128)(2,1)S(1)}, u32[]{:S(2)}, u32[]{:S(2)}) collective-permute-start(bf16[24,1024]{1,0:T(8,128)(2,1)S(1)} %get-tuple-element.10.own_ref), channel_id=1, source_target_pairs={{0,1},{1,0},{2,3},{3,2},{4,5},{5,4},{6,7},{7,6},{8,9},{9,8},{10,11... | collective-permute-start | bytes 147464 | tf_op jit(solution)/shard_map/ppermute | solution.py:399
  10.2 3.8 %collective-permute-start.4 = (f32[1,24,512]{2,1,0:T(8,128)S(1)}, f32[1,24,512]{2,1,0:T(8,128)S(1)}, u32[]{:S(2)}, u32[]{:S(2)}) collective-permute-start(f32[1,24,512]{2,1,0:T(8,128)S(1)} %bitcast.3), channel_id=1, source_target_pairs={{0,3},{1,2},{2,1},{3,0},{4,7},{5,6},{6,5},{7,4},{8,11},{9,10},{10,... | collective-permute-start | bytes 147464 | tf_op jit(solution)/shard_map/ppermute | solution.py:440
  12.2 1.8 %collective-permute-start.3 = (f32[1,24,512]{2,1,0:T(8,128)S(1)}, f32[1,24,512]{2,1,0:T(8,128)S(1)}, u32[]{:S(2)}, u32[]{:S(2)}) collective-permute-start(f32[1,24,512]{2,1,0:T(8,128)S(1)} %bitcast.4), channel_id=1, source_target_pairs={{0,1},{1,0},{2,3},{3,2},{4,5},{5,4},{6,7},{7,6},{8,9},{9,8},{10,11... | collective-permute-start | bytes 147464 | tf_op jit(solution)/shard_map/ppermute | solution.py:440
  14.0 1.5 %collective-permute-start.5 = (f32[1,8,512]{2,1,0:T(8,128)S(1)}, f32[1,8,512]{2,1,0:T(8,128)S(1)}, u32[]{:S(2)}, u32[]{:S(2)}) collective-permute-start(f32[1,8,512]{2,1,0:T(8,128)S(1)} %shard_map.66.own_ref), channel_id=1, source_target_pairs={{0,1},{1,0},{2,3},{3,2},{4,5},{5,4},{6,7},{7,6},{8,9},{9,8},{10,11... | collective-permute-start | bytes 49160 | tf_op jit(solution)/shard_map/ppermute | solution.py:399
